TPU v7x, 256 devices: a whole 4x4x8 slice. The times are simulated.
256 devices in a mesh: bx: 4 (over y_hi, core), by: 8 (over y_lo, x), bz: 8 (over z).
Axes of the slice: x: 4, y: 4 (y_hi: 2, y_lo: 2; y = y_hi * 2 + y_lo), z: 8, core: 2. Of those that a mesh axis runs over, the one named last changes fastest.
Arguments:
- space_factor: float32 [64, 8, 64, 1024], P(None, 'bx', 'by', 'bz'), may hold values from -6 to 6
- core_matrix: float32 [64, 64], replicated, may hold values from -0.1 to 3
- velocity_factor: float32 [64, 32768], P(None, ('bx', 'by')), may hold values from -30 to 30
Outputs:
- new_space: float32 [64, 8, 64, 1024], P(None, 'bx', 'by', 'bz')
- new_core: float32 [64, 64], replicated
- new_velocity: float32 [64, 32768], P(None, ('bx', 'by'))
All inputs are finite; a program needn't handle non-finite values.
Results may differ from a plain program's by a relative error of at most 0.0028.
Values sent between devices are 32-bit elements; how exact they have to be, the bound alone decides.
No kernel may reach another device: no remote copies, remote signals or barrier semaphores. Data moves between devices by JAX's collectives and lax.ppermute only.
A program may use at most 64 MiB of HBM per device.

v0:
```python
import functools

import jax
import jax.numpy as jnp
import numpy as np
from jax import lax
from jax.experimental import pallas as pl
from jax.experimental.pallas import tpu as pltpu
from jax.sharding import PartitionSpec as P

VEL_N = 32
STEPS = 2
TIME_STEP = 0.1
SPEED_MAX = 3.0
HIGHEST = lax.Precision.HIGHEST
PLANE = ("bx", "by")
RANK = 64
F32 = jnp.float32


def mm(a, b):
    return jnp.dot(a, b, precision=HIGHEST, preferred_element_type=F32)


def mmt(a, b):
    return lax.dot_general(
        a, b, (((1,), (1,)), ((), ())), precision=HIGHEST, preferred_element_type=F32
    )


def np_tables(row_total):
    row_ids = np.arange(row_total)
    levels = np.stack([row_ids // (VEL_N * VEL_N), row_ids // VEL_N % VEL_N, row_ids % VEL_N])
    v = SPEED_MAX * (2.0 * levels + 1.0 - VEL_N) / VEL_N
    w = np.exp(-0.5 * np.sum(v * v, axis=0)) / line_mean() ** 3
    modes = np.stack(
        [w, w * v[0], w * v[1], w * v[2]]
        + [0.5 * w * (v[d] * v[d] - 1.0) for d in range(3)]
        + [w * v[0] * v[1], w * v[0] * v[2], w * v[1] * v[2]]
    )
    weights = [np.ones_like(w)]
    for d in range(3):
        weights += [np.maximum(v[d], 0.0), np.minimum(v[d], 0.0)]
    return v, modes, np.stack(weights)


def line_mean():
    line = SPEED_MAX * (2.0 * np.arange(VEL_N) + 1.0 - VEL_N) / VEL_N
    return float(np.mean(np.exp(-0.5 * line * line)))


def constants(row_total):
    v, modes, weights = np_tables(row_total)
    gram = np.einsum("wv,mv,nv->wmn", weights, modes, modes)
    out = np.zeros((160, 16), np.float32)
    for w in range(7):
        out[16 * w : 16 * w + 10, :10] = gram[w]
    out[112, :10] = modes.sum(axis=1)
    for d in range(3):
        out[113 + d, :10] = modes @ v[d]
    first = [0, 1, 2, 3, 1, 2, 3, 1, 1, 2]
    second = [None, None, None, None, 1, 2, 3, 2, 3, 3]
    for r in range(10):
        out[120 + r, first[r]] = 1.0
        if second[r] is not None:
            out[136 + r, second[r]] = 1.0
    return out


def iota(shape, dim):
    return lax.broadcasted_iota(jnp.int32, shape, dim)


def eye():
    return (iota((RANK, RANK), 0) == iota((RANK, RANK), 1)).astype(F32)


def spread_lane(block, k):
    return jnp.broadcast_to(block[:, k : k + 1], (8, 128))


def spread_row(block, r):
    return jnp.broadcast_to(block[r : r + 1, :], (8, 128))


def chol_inverse(gram, width=4):
    lane = iota((8, 128), 1)
    sub = iota((8, 128), 0)
    on_diag = gram * eye()
    diag = jnp.sum(on_diag, axis=0, keepdims=True)
    row_scale = lax.rsqrt(diag)
    scaled = gram * row_scale * lax.rsqrt(jnp.sum(on_diag, axis=1, keepdims=True))
    wide = jnp.concatenate([scaled, jnp.zeros_like(gram)], axis=1)
    blocks = []
    for b in range(8):
        unit = jnp.where(lane == sub + (64 + 8 * b), 1.0, 0.0)
        blocks.append(wide[8 * b : 8 * b + 8] + unit)
    for k in range(0, RANK, width):
        b, r = divmod(k, 8)
        left = range(b, 8)
        cols = [{i: spread_lane(blocks[i], k + j) for i in left} for j in range(width)]
        heads = [spread_row(blocks[b], r + j) for j in range(width)]
        for j in range(0, width, 2):
            p = spread_row(cols[j][b], r + j)
            q = spread_row(cols[j][b], r + j + 1)
            s = spread_row(cols[j + 1][b], r + j + 1)
            inv_p = lax.rsqrt(p)
            both = inv_p * lax.rsqrt(p * s - q * q)
            pb, qb = both * p, both * q
            for i in left:
                first = cols[j][i]
                cols[j][i] = first * inv_p
                cols[j + 1][i] = pb * cols[j + 1][i] - qb * first
            first = heads[j]
            heads[j] = first * inv_p
            heads[j + 1] = pb * heads[j + 1] - qb * first
            for m in range(j + 2, width):
                u = spread_row(cols[j][b], r + m)
                w = spread_row(cols[j + 1][b], r + m)
                for i in left:
                    cols[m][i] = (cols[m][i] - cols[j][i] * u) - cols[j + 1][i] * w
                heads[m] = (heads[m] - heads[j] * u) - heads[j + 1] * w
        for i in left:
            if i == b and r + width == 8:
                new = blocks[i]
            else:
                new = blocks[i]
                for j in range(width):
                    new = new - cols[j][i] * heads[j]
            if i == b:
                new = jnp.where(sub >= r + width, new, blocks[i])
                for j in range(width):
                    new = jnp.where(sub == r + j, heads[j], new)
            blocks[i] = new
    full = jnp.concatenate(blocks, axis=0)
    keep = iota((RANK, RANK), 1) >= iota((RANK, RANK), 0)
    upper = jnp.where(keep, full[:, :RANK], 0.0) * (diag * row_scale)
    return upper, full[:, RANK:] * row_scale


def features(sel_map, field):
    both = mm(sel_map, field)
    lift = jnp.where(iota((16, field.shape[1]), 0) < 4, 1.0, 0.0)
    return both[:16] * (both[16:] + lift)


def pair_block(plus, minus):
    return jnp.where(iota((RANK, RANK), 0) <= iota((RANK, RANK), 1), plus, minus)


def tables_kernel(v1_ref, tab_ref):
    lanes = tab_ref.shape[1]
    at = iota((1, lanes), 1)
    v2 = SPEED_MAX * (2.0 * (at // VEL_N).astype(F32) + 1.0 - VEL_N) / VEL_N
    v3 = SPEED_MAX * (2.0 * (at % VEL_N).astype(F32) + 1.0 - VEL_N) / VEL_N
    v1 = jnp.full((1, lanes), v1_ref[0, 0], F32)
    w = jnp.exp(-0.5 * (v1 * v1 + v2 * v2 + v3 * v3)) / (line_mean() ** 3)
    tab_ref[...] = jnp.zeros_like(tab_ref)
    modes = [w, w * v1, w * v2, w * v3]
    modes += [0.5 * w * (v * v - 1.0) for v in (v1, v2, v3)]
    modes += [w * v1 * v2, w * v1 * v3, w * v2 * v3]
    for i, m in enumerate(modes):
        tab_ref[i : i + 1, :] = m
    for i, m in enumerate([jnp.ones_like(v1), v1, v2, v3]):
        tab_ref[16 + i : 17 + i, :] = m


def weigh_kernel(scale, v1_ref, rows_ref, tab_ref, coll_ref, out_ref, stack_ref, res_ref):
    v1 = v1_ref[0, 0]
    lanes = rows_ref.shape[1]
    width = lanes // 4
    res_ref[...] = jnp.zeros_like(res_ref)

    def chunk(c, carry):
        cols = pl.ds(pl.multiple_of(c * width, width), width)
        rows, modes = rows_ref[:, cols], tab_ref[0:16, cols]
        v2, v3 = tab_ref[18:19, cols], tab_ref[19:20, cols]
        weights = [None, jnp.maximum(v2, 0.0), jnp.minimum(v2, 0.0)]
        weights += [jnp.maximum(v3, 0.0), jnp.minimum(v3, 0.0)]
        for i, w in enumerate(weights):
            stack_ref[80 * i : 80 * i + 64, :] = rows if w is None else rows * w
            stack_ref[80 * i + 64 : 80 * i + 80, :] = modes if w is None else modes * w
        stack_ref[400:408, :] = tab_ref[16:24, cols]
        res_ref[...] += mmt(stack_ref[...], rows)
        return carry

    lax.fori_loop(0, 4, chunk, 0)
    quads = [res_ref[80 * i : 80 * i + 64, :] * scale for i in range(5)]
    cross = [res_ref[80 * i + 64 : 80 * i + 80, :] * scale for i in range(5)]
    out_ref[...] = jnp.zeros_like(out_ref)
    out_ref[0:64, 0:64] = quads[0]
    out_ref[128:144, 0:64] = cross[0]
    v1p, v1m = jnp.maximum(v1, 0.0), jnp.minimum(v1, 0.0)
    pairs = [(quads[0] * v1p, quads[0] * v1m), (quads[1], quads[2]), (quads[3], quads[4])]
    crosses = [cross[0] * v1p, cross[0] * v1m] + cross[1:]
    out_ref[0:64, 64:128] = pair_block(*pairs[1])
    out_ref[64:128, 0:64] = pair_block(*pairs[0])
    out_ref[64:128, 64:128] = pair_block(*pairs[2])
    for i in range(6):
        out_ref[144 + 16 * i : 160 + 16 * i, 0:64] = crosses[i]
    out_ref[128:136, 64:128] = res_ref[400:408, :] * scale
    out_ref[136:152, 64:128] = coll_ref[...]
    for d in range(3):
        out_ref[152 + d : 153 + d, 64:128] = jnp.sum(pairs[d][1] * eye(), axis=0, keepdims=True)


def symmetric(sums, gain, cons):
    upper = iota((RANK, RANK), 0) <= iota((RANK, RANK), 1)
    diag = iota((RANK, RANK), 0) == iota((RANK, RANK), 1)
    packs = [sums[64:128, 0:64], sums[0:64, 64:128], sums[64:128, 64:128]]
    grams = [sums[0:64, 0:64]]
    for d in range(3):
        turned = packs[d].T
        grams.append(jnp.where(upper, packs[d], turned))
        grams.append(
            jnp.where(diag, sums[152 + d : 153 + d, 64:128], jnp.where(upper, turned, packs[d]))
        )
    mode_gain = mmt(cons[0:120], gain)
    for w in range(7):
        half = sums[128 + 16 * w : 144 + 16 * w, 0:64] + 0.5 * mode_gain[16 * w : 16 * w + 16]
        cross = mm(gain, half)
        grams[w] = grams[w] + (cross + cross.T)
    mode_rows = sums[128:144, 0:64] + mode_gain[0:16]
    moments = sums[128:136, 64:128] + mode_gain[112:120]
    return grams, mode_rows, moments


def shifted_stack(p, stack_ref, mine, lower, upper, yl_ref, yh_ref, zl_ref, zh_ref):
    lane = iota((RANK, 128), 1)
    field = mine[...]
    stack_ref[0:64, :] = field
    stack_ref[64:128, :] = lower[...]
    stack_ref[256:320, :] = upper[...]
    n = field.shape[1] // 128
    zl, zh = zl_ref[...], zh_ref[...]
    for y in range(n):
        here = field[:, 128 * y : 128 * y + 128]
        cols = slice(128 * y, 128 * y + 128)
        halo = slice(128 * p, 128 * p + 128)
        stack_ref[128:192, cols] = yl_ref[:, halo] if y == 0 else field[:, 128 * (y - 1) : 128 * y]
        stack_ref[320:384, cols] = (
            yh_ref[:, halo] if y == n - 1 else field[:, 128 * (y + 1) : 128 * (y + 2)]
        )
        g = p * n + y
        low = pltpu.roll(zl, (128 - g) % 128, 1)
        stack_ref[192:256, cols] = jnp.where(lane == 0, low, pltpu.roll(here, 1, 1))
        high = pltpu.roll(zh, 127 - g, 1)
        stack_ref[384:448, cols] = jnp.where(lane == 127, high, pltpu.roll(here, 127, 1))


def maps_kernel(
    count, cells, sums_ref, base_ref, cons_ref, fa, fb, xh, yl, yh, zl, zh,
    kb_ref, map_ref, sel_ref, seln_ref, gw_ref, mode_ref, mom_ref, civ_ref, ginv_ref, gain_ref,
    stack_ref,
):
    sums, base, cons = sums_ref[...], base_ref[...], cons_ref[...]
    gain = (TIME_STEP / cells) * mmt(base, sums[136:152, 64:128])
    gain_ref[...] = gain
    grams, mode_rows, moments = symmetric(sums, gain, cons)
    shifted_stack(1, stack_ref, fb, fa, xh, yl, yh, zl, zh)
    sides = mm(jnp.concatenate(grams, axis=0), base)
    sides = [sides[64 * w : 64 * w + 64] for w in range(7)]
    stay = (1.0 - TIME_STEP) * sides[0]
    for d in range(3):
        stay = stay + TIME_STEP * (sides[2 * d + 2] - sides[2 * d + 1])
    row = [stay] + [TIME_STEP * sides[2 * d + 1] for d in range(3)]
    row += [-TIME_STEP * sides[2 * d + 2] for d in range(3)] + [TIME_STEP * mode_rows.T]
    row = jnp.concatenate(row, axis=1) * (1.0 / count)
    sel = mm(cons[120:152, 0:8], mm(moments, base) * (1.0 / count))
    sel_ref[...] = sel
    stack_ref[448:464, :] = features(sel, fb[...])
    gw_ref[...] = jnp.concatenate(grams[1:], axis=1)
    mode_ref[...] = mode_rows
    mom_ref[...] = moments
    _, civ = chol_inverse(grams[0] * (1.0 / count))
    maps = mm(civ, row)
    kb_ref[...] = mm(maps, stack_ref[...])
    map_ref[...] = maps
    civ_ref[...] = civ
    ginv_ref[...] = mm(civ.T, civ) * (1.0 / count)
    seln_ref[...] = mm(cons[120:152, 0:8], mmt(moments, civ) * (1.0 / count))


def columns(fields, lane_at):
    lane = iota((RANK, 128), 1)
    out = jnp.zeros((RANK, 128), F32)
    g = 0
    for field in fields:
        for y in range(field.shape[1] // 128):
            here = field[:, 128 * y : 128 * y + 128]
            out = jnp.where(lane == g, pltpu.roll(here, (g - lane_at) % 128, 1), out)
            g += 1
    return out


def plane_kernel(
    map_ref, sel_ref, fa, fb, xl, yl, yh, zl, zh, kb,
    ka_ref, ylo_ref, yho_ref, zlo_ref, zho_ref, stack_ref,
):
    shifted_stack(0, stack_ref, fa, xl, fb, yl, yh, zl, zh)
    stack_ref[448:464, :] = features(sel_ref[...], fa[...])
    ka = mm(map_ref[...], stack_ref[...])
    ka_ref[...] = ka
    kb = kb[...]
    n = ka.shape[1]
    ylo_ref[...] = jnp.concatenate([ka[:, n - 128 :], kb[:, n - 128 :]], axis=1)
    yho_ref[...] = jnp.concatenate([ka[:, :128], kb[:, :128]], axis=1)
    zlo_ref[...] = columns((ka, kb), 127)
    zho_ref[...] = columns((ka, kb), 0)


def inner_kernel(seln_ref, ka, kb, out_ref, stack_ref):
    lane = iota((RANK, 128), 1)
    n = ka.shape[1]
    zero = jnp.zeros((RANK, 128), F32)
    for p, ref in enumerate((ka, kb)):
        at = p * n
        field = ref[...]
        stack_ref[0:64, at : at + n] = field
        stack_ref[128:192, at : at + 128] = zero
        stack_ref[128:192, at + 128 : at + n] = field[:, : n - 128]
        for y in range(n // 128):
            here = field[:, 128 * y : 128 * y + 128]
            stack_ref[192:256, at + 128 * y : at + 128 * y + 128] = jnp.where(
                lane == 0, 0.0, pltpu.roll(here, 1, 1)
            )
        stack_ref[256:272, at : at + n] = features(seln_ref[...], field)
    stack_ref[64:128, 0:n] = jnp.zeros((RANK, n), F32)
    stack_ref[64:128, n : 2 * n] = ka[...]
    out_ref[...] = jnp.zeros_like(out_ref)
    width = n // 2

    def chunk(c, carry):
        cols = pl.ds(pl.multiple_of(c * width, width), width)
        out_ref[...] += mmt(stack_ref[:, cols], stack_ref[0:64, cols])
        return carry

    lax.fori_loop(0, 4, chunk, 0)


def edge_kernel(part_ref, ka, xl, yl, yh, zl, zh, out_ref):
    part = part_ref[...]
    out_ref[0:64, 0:64] = part[0:64]
    out_ref[32:48, 0:32] = part[256:272, 0:32]
    out_ref[48:64, 0:32] = part[256:272, 32:64]
    out_ref[0:64, 64:128] = part[64:128] + mmt(xl[...], ka[...])
    out_ref[64:128, 0:64] = part[128:192] + mmt(yl[...], yh[...])
    out_ref[64:128, 64:128] = part[192:256] + mmt(zl[...], zh[...])


def core_kernel(
    count, cells, v1_ref, sums_ref, ka, kb, rows_ref, gain_ref, tab_ref, cons_ref,
    gw_ref, mode_ref, mom_ref, civ_ref, ginv_ref, coll_ref, rows_out, cxi_ref, base_ref,
):
    v1 = v1_ref[0, 0]
    rows = rows_ref[...] + mm(gain_ref[...], tab_ref[0:16, :])
    v2, v3 = tab_ref[18:19, :], tab_ref[19:20, :]
    base_ref[0:64, :] = rows
    base_ref[64:128, :] = rows * jnp.maximum(v2, 0.0)
    base_ref[128:192, :] = rows * jnp.minimum(v2, 0.0)
    base_ref[192:256, :] = rows * jnp.maximum(v3, 0.0)
    base_ref[256:320, :] = rows * jnp.minimum(v3, 0.0)
    sums = sums_ref[...] * (1.0 / cells)
    civ = civ_ref[...]
    unit = eye()
    gram = sums[0:64, 0:64]
    corner = (iota((RANK, RANK), 0) >= 32) & (iota((RANK, RANK), 1) < 32)
    up, cxi = chol_inverse(jnp.where(corner, gram.T, gram))
    cxi_ref[...] = cxi
    moment_x = jnp.concatenate([sums[32:48, 0:32], sums[48:64, 0:32]], axis=1)
    y = mm(up, civ)
    zs = jnp.concatenate([sums[0:64, 64:128], sums[64:128, 0:64], sums[64:128, 64:128]], axis=0)
    zs = mmt(zs, cxi)
    lower, upper = [], []
    for d in range(3):
        turned = mm(cxi, zs[64 * d : 64 * d + 64])
        lower.append(unit - turned.T)
        upper.append(turned - unit)
    yg = mm(y, gw_ref[...])
    yg = jnp.concatenate([yg[:, 64 * w : 64 * w + 64] for w in range(6)], axis=0)
    sides = jnp.concatenate([lower[0], upper[0], lower[1], upper[1], lower[2], upper[2]], axis=1)
    rate = mm(mmt(cxi, moment_x), mode_ref[...]) - mm(sides, yg)
    y = (1.0 + TIME_STEP) * y - TIME_STEP * mm(rate, ginv_ref[...])
    sel = mm(cons_ref[120:152, 0:8], mm(mmt(mom_ref[...], y) * (1.0 / count), cxi))
    collide = mmt(features(sel, ka[...]), ka[...]) + mmt(features(sel, kb[...]), kb[...])
    turn = lower[0] * jnp.maximum(v1, 0.0) + upper[0] * jnp.minimum(v1, 0.0)
    move = [(1.0 - TIME_STEP) * unit - TIME_STEP * turn]
    move += [-TIME_STEP * m for m in (lower[1], upper[1], lower[2], upper[2])]
    move = mm(jnp.concatenate(move, axis=0), y)
    move = jnp.concatenate([move[64 * t : 64 * t + 64] for t in range(5)], axis=1)
    rows_out[...] = mm(move, base_ref[...])
    coll_ref[...] = collide


def finish_kernel(count, cells, sums_ref, cxi_ref, rows_ref, tab_ref, cons_ref, low_ref, out_ref):
    sums = sums_ref[...]
    gain = (TIME_STEP / cells) * mmt(cxi_ref[...], sums[136:152, 64:128])
    half = sums[128:144, 0:64] + 0.5 * mmt(cons_ref[0:16, :], gain)
    cross = mm(gain, half)
    up, civ = chol_inverse((sums[0:64, 0:64] + (cross + cross.T)) * (1.0 / count))
    low_ref[...] = up.T
    out_ref[...] = mm(civ, rows_ref[...] + mm(gain, tab_ref[0:16, :]))


def call(kernel, outs, scratch, *args):
    shapes = [jax.ShapeDtypeStruct(s, F32) for s in outs]
    specs = [pl.BlockSpec(memory_space=pltpu.VMEM) for _ in args]
    if args[0].shape == (1, 1):
        specs[0] = pl.BlockSpec(memory_space=pltpu.SMEM)
    return pl.pallas_call(
        kernel,
        out_shape=shapes,
        in_specs=specs,
        out_specs=[pl.BlockSpec(memory_space=pltpu.VMEM) for _ in outs],
        scratch_shapes=[pltpu.VMEM(s, F32) for s in scratch],
        compiler_params=pltpu.CompilerParams(vmem_limit_bytes=40 * 1024 * 1024),
    )(*args)


def route(axis, step):
    n = lax.axis_size(axis)
    return [(i, (i + step) % n) for i in range(n)]


def swap(chunks, axis):
    return lax.all_to_all(chunks, axis, 0, 0, tiled=True)


def spread(part, n):
    return jnp.broadcast_to(part[None], (n,) + part.shape)


def plane_sum(payload):
    n = lax.axis_size(PLANE)
    return jnp.sum(swap(payload.reshape(n, -1, 128), PLANE), axis=0)


def line_sum(part):
    return jnp.sum(swap(spread(part, lax.axis_size("bz")), "bz"), axis=0)


def plane_gather(part):
    return swap(spread(part, lax.axis_size(PLANE)), PLANE).reshape(-1, 128)


def local(space_factor, core_matrix, velocity_factor):
    vel_rows = velocity_factor.shape[1]
    plane = lax.axis_index(PLANE)
    count = vel_rows * lax.axis_size(PLANE)
    nz = lax.axis_size("bz")
    shape = space_factor.shape
    half = shape[2] * shape[3]
    cells = 2 * half * lax.axis_size(PLANE) * nz
    cons = jnp.asarray(constants(count))
    digit = (plane * vel_rows) // (VEL_N * VEL_N)
    v1 = SPEED_MAX * (2.0 * digit.astype(F32) + 1.0 - VEL_N) / VEL_N
    v1 = v1.reshape(1, 1)

    fa = space_factor[:, 0].reshape(RANK, half)
    fb = space_factor[:, 1].reshape(RANK, half)
    (tab,) = call(tables_kernel, [(24, vel_rows)], [], v1)

    def weigh(rows, coll, scale):
        return call(
            functools.partial(weigh_kernel, scale),
            [(256, 128)], [(408, vel_rows // 4), (408, RANK)], v1, rows, tab, coll,
        )[0]

    payload = weigh(velocity_factor, jnp.zeros((16, RANK), F32), 1.0)
    yl = space_factor[:, :, -1].reshape(RANK, 256)
    yh = space_factor[:, :, 0].reshape(RANK, 256)
    pad = jnp.zeros((RANK, 128 - 2 * shape[2]), F32)
    zl = jnp.concatenate([space_factor[:, :, :, -1].reshape(RANK, -1), pad], axis=1)
    zh = jnp.concatenate([space_factor[:, :, :, 0].reshape(RANK, -1), pad], axis=1)

    def low_halo(xl, yl, zl):
        return (
            lax.ppermute(xl, "bx", route("bx", 1)),
            lax.ppermute(yl, "by", route("by", 1)),
            lax.ppermute(zl, "bz", route("bz", 1)),
        )

    def high_halo(xh, yh, zh):
        return (
            lax.ppermute(xh, "bx", route("bx", -1)),
            lax.ppermute(yh, "by", route("by", -1)),
            lax.ppermute(zh, "bz", route("bz", -1)),
        )

    low = low_halo(fb, yl, zl)
    high = high_halo(fa, yh, zh)
    sums = plane_gather(plane_sum(payload))

    def step(turn, carry):
        fa, fb, low, high, sums, rows, base = carry
        kb, maps, sel, seln, gw, mode_rows, moments, civ, ginv, gain = call(
            functools.partial(maps_kernel, count, cells),
            [(RANK, half), (RANK, 464), (32, RANK), (32, RANK), (RANK, 384), (16, RANK), (8, RANK),
             (RANK, RANK), (RANK, RANK), (RANK, 16)],
            [(464, half)],
            sums, base, cons, fa, fb, high[0], low[1], high[1], low[2], high[2],
        )
        ka, yl, yh, zl, zh = call(
            plane_kernel,
            [(RANK, half), (RANK, 256), (RANK, 256), (RANK, 128), (RANK, 128)],
            [(464, half)],
            maps, sel, fa, fb, low[0], low[1], high[1], low[2], high[2], kb,
        )
        low = low_halo(kb, yl, zl)
        (part,) = call(inner_kernel, [(272, RANK)], [(272, 2 * half)], seln, ka, kb)
        (payload,) = call(edge_kernel, [(128, 128)], [], part, ka, low[0], low[1], yh, low[2], zh)
        high = high_halo(ka, yh, zh)
        sums = plane_gather(line_sum(plane_sum(payload)))
        coll, rows, base = call(
            functools.partial(core_kernel, count, cells),
            [(16, RANK), (RANK, vel_rows), (RANK, RANK)],
            [(320, vel_rows)],
            v1, sums, ka, kb, rows, gain, tab, cons, gw, mode_rows, moments, civ, ginv,
        )
        sums = plane_gather(line_sum(plane_sum(weigh(rows, coll, 1.0 / nz))))
        return ka, kb, low, high, sums, rows, base

    carry = (fa, fb, low, high, sums, velocity_factor, core_matrix.T)
    ka, kb, _, _, sums, rows, base = lax.fori_loop(0, STEPS, step, carry)
    new_space = jnp.stack(
        [mm(base, ka).reshape(RANK, *shape[2:]), mm(base, kb).reshape(RANK, *shape[2:])], axis=1
    )
    new_core, new_velocity = call(
        functools.partial(finish_kernel, count, cells),
        [(RANK, RANK), (RANK, vel_rows)], [], sums, base, rows, tab, cons,
    )
    return new_space, new_core, new_velocity


def solution(mesh):
    return jax.shard_map(
        local,
        mesh=mesh,
        in_specs=(P(None, "bx", "by", "bz"), P(), P(None, PLANE)),
        out_specs=(P(None, "bx", "by", "bz"), P(), P(None, PLANE)),
        check_vma=False,
    )
```

profile of v0, /device:TPU:1, one launch (start us, length us, event | category | flops | bytes accessed | tf_op | source)
XLA Modules:
  0.0 237.9 jit_solution(14949981091392794403)
XLA Ops:
  0.6 1.0 copy.88.rows_ref
  2.1 2.1 collective-permute-start.7
  4.3 2.7 %shard_map.68 = f32[256,128]{1,0:T(8,128)} custom-call(f32[1,1]{1,0:T(1,128)} %bitcast.2.v1_ref, f32[64,1024]{1,0:T(8,128)S(1)} %copy.88.rows_ref, f32[24,1024]{1,0:T(8,128)S(1)} %shard_map.67.tab_ref, f32[16,64]{1,0:T(8,128)S(1)} %broadcast_in_dim.12.coll_ref), custom_call_target="tpu_custom_call" | custom-call | tf_op jit(solution)/shard_map/pallas_call | solution.py:410
  7.1 7.8 %all-to-all-start.6 = ((f32[32,8,128]{2,1,0:T(8,128)}), f32[32,8,128]{2,1,0:T(8,128)S(1)}, u32[]{:S(2)}, u32[]{:S(2)}) async-start(f32[32,8,128]{2,1,0:T(8,128)} %bitcast.3), calls=%async_computation.6 | async-start | bytes 262144 | tf_op jit(solution)/shard_map/all_to_all | solution.py:426
  15.3 3.1 %collective-permute-start.6 = (f32[64,1024]{1,0:T(8,128)S(1)}, f32[64,1024]{1,0:T(8,128)S(1)}, u32[]{:S(2)}, u32[]{:S(2)}) collective-permute-start(f32[64,1024]{1,0:T(8,128)S(1)} %bitcast.58), channel_id=1, source_target_pairs={{0,64},{64,128},{128,192},{192,0},{1,65},{65,129},{129,193},{193,1... | collective-permute-start | bytes 786440 | tf_op jit(solution)/shard_map/ppermute | solution.py:478
  18.4 4.0 %all-to-all-done.6 = f32[32,8,128]{2,1,0:T(8,128)S(1)} async-done(((f32[32,8,128]{2,1,0:T(8,128)}), f32[32,8,128]{2,1,0:T(8,128)S(1)}, u32[]{:S(2)}, u32[]{:S(2)}) %all-to-all-start.6) | async-done | bytes 131104 | tf_op jit(solution)/shard_map/all_to_all | solution.py:426
  23.1 4.0 %all-to-all-start.7 = ((f32[32,8,128]{2,1,0:T(8,128)}), f32[32,8,128]{2,1,0:T(8,128)S(1)}, u32[]{:S(2)}, u32[]{:S(2)}) async-start(f32[32,8,128]{2,1,0:T(8,128)} %broadcast_in_dim.13), calls=%async_computation.7 | async-start | bytes 262144 | tf_op jit(solution)/shard_map/all_to_all | solution.py:426
  27.6 5.6 %collective-permute-start.11 = (f32[64,128]{0,1:T(8,128)S(1)}, f32[64,128]{0,1:T(8,128)S(1)}, u32[]{:S(2)}, u32[]{:S(2)}) collective-permute-start(f32[64,128]{0,1:T(8,128)S(1)} %concatenate.7), channel_id=1, source_target_pairs={{0,7},{1,0},{2,1},{3,2},{4,3},{5,4},{6,5},{7,6},{8,15},{9,8},{10,9... | collective-permute-start | bytes 98312 | tf_op jit(solution)/shard_map/ppermute | solution.py:487
  33.2 3.5 %collective-permute-start.10 = (f32[64,256]{1,0:T(8,128)S(1)}, f32[64,256]{1,0:T(8,128)S(1)}, u32[]{:S(2)}, u32[]{:S(2)}) collective-permute-start(f32[64,256]{1,0:T(8,128)S(1)} %bitcast.70), channel_id=1, source_target_pairs={{0,56},{8,0},{16,8},{24,16},{32,24},{40,32},{48,40},{56,48},{1,57}... | collective-permute-start | bytes 196616 | tf_op jit(solution)/shard_map/ppermute | solution.py:486
  37.9 3.5 %collective-permute-done.8 = f32[64,128]{0,1:T(8,128)S(1)} collective-permute-done((f32[64,128]{0,1:T(8,128)S(1)}, f32[64,128]{0,1:T(8,128)S(1)}, u32[]{:S(2)}, u32[]{:S(2)}) %collective-permute-start.8) | collective-permute-done | bytes 32800 | tf_op jit(solution)/shard_map/ppermute | solution.py:480
  41.6 190.1 %while.31 = (s32[]{:T(128)}, f32[64,1024]{1,0:T(8,128)S(1)}, f32[64,1024]{1,0:T(8,128)S(1)}, f32[64,1024]{1,0:T(8,128)S(1)}, f32[64,256]{1,0:T(8,128)S(1)}, /*in...) while((s32[]{:T(128)}, f32[64,1024]{1,0:T(8,128)S(1)}, ...), condition=%wide.region_6.7_spmd.clone, body=%wide.region_1.6_spmd.sunk.clone.sunk | while | flops 58370 | bytes 6709757 | solution.py:524
  41.8 5.4 %eval_jaxpr.6 = (f32[64,1024]{1,0:T(8,128)S(1)}, f32[64,464]{1,0:T(8,128)S(1)}, f32[32,64]{1,0:T(8,128)S(1)}, f32[32,64]{1,0:T(8,128)S(1)}, f32[64,384]{1,0:T(8,...) custom-call(f32[256,128]{1,0:T(8,128)S(1)} %get-tuple-element.415.su, ...), custom_call_target="tpu_custom_call" | custom-call | tf_op jit(solution)/shard_map/while/body/eval_jaxpr/pallas_call | solution.py:410
  47.2 4.5 %collective-permute-start = (f32[64,1024]{1,0:T(8,128)S(1)}, f32[64,1024]{1,0:T(8,128)S(1)}, u32[]{:S(2)}, u32[]{:S(2)}) collective-permute-start(f32[64,1024]{1,0:T(8,128)S(1)} %get-tuple-element.425.kb), channel_id=1, source_target_pairs={{0,64},{64,128},{128,192},{192,0},{1,65},{65,129},{129,193},{193,1... | collective-permute-start | bytes 786440 | tf_op jit(solution)/shard_map/while/body/eval_jaxpr/ppermute | solution.py:478
  51.7 1.3 eval_jaxpr.7
  53.2 2.8 %eval_jaxpr.8.part_ref = f32[272,64]{1,0:T(8,128)S(1)} custom-call(f32[32,64]{1,0:T(8,128)S(1)} %get-tuple-element.379.seln_ref, f32[64,1024]{1,0:T(8,128)S(1)} %get-tuple-element.424.ka, f32[64,1024]{1,0:T(8,128)S(1)} %get-tuple-element.425.kb), custom_call_target="tpu_custom_call" | custom-call | tf_op jit(solution)/shard_map/while/body/eval_jaxpr/pallas_call | solution.py:410
  56.0 1.1 collective-permute-done.2.zl
  57.1 1.2 collective-permute-done.1.yl
  58.8 12.0 %all_to_all.58 = f32[32,4,128]{2,1,0:T(4,128)S(1)} all-to-all(f32[32,4,128]{2,1,0:T(4,128)S(1)} %bitcast.54), channel_id=1, replica_groups=mesh['bx'=4,'by'=8,'bz'=8] {'bx','by'}, dimensions={0} | all-to-all | bytes 131072 | tf_op jit(solution)/shard_map/while/body/eval_jaxpr/all_to_all | solution.py:426
  70.9 9.7 %all_to_all.59 = f32[8,4,128]{2,1,0:T(4,128)S(1)} all-to-all(f32[8,4,128]{2,1,0:T(4,128)S(1)} %broadcast_in_dim.48), channel_id=1, replica_groups=mesh['bx'=4,'by'=8,'bz'=8] {'bz'}, dimensions={0} | all-to-all | bytes 32768 | tf_op jit(solution)/shard_map/while/body/eval_jaxpr/all_to_all | solution.py:426
  81.3 5.4 %all-to-all-start.2 = ((f32[32,4,128]{2,1,0:T(4,128)}), f32[32,4,128]{2,1,0:T(4,128)S(1)}, u32[]{:S(2)}, u32[]{:S(2)}) async-start(f32[32,4,128]{2,1,0:T(4,128)} %broadcast_in_dim.49), calls=%async_computation.2 | async-start | bytes 131072 | tf_op jit(solution)/shard_map/while/body/eval_jaxpr/all_to_all | solution.py:426
  86.7 7.3 %all-to-all-done.2 = f32[32,4,128]{2,1,0:T(4,128)S(1)} async-done(((f32[32,4,128]{2,1,0:T(4,128)}), f32[32,4,128]{2,1,0:T(4,128)S(1)}, u32[]{:S(2)}, u32[]{:S(2)}) %all-to-all-start.2) | async-done | bytes 65568 | tf_op jit(solution)/shard_map/while/body/eval_jaxpr/all_to_all | solution.py:426
  94.0 6.9 %eval_jaxpr.10 = (f32[16,64]{1,0:T(8,128)S(1)}, f32[64,1024]{1,0:T(8,128)S(1)}, f32[64,64]{1,0:T(8,128)S(1)}) custom-call(f32[1,1]{1,0:T(1,128)} %get-tuple-element.435.v1_ref, f32[128,128]{1,0:T(8,128)S(1)} %bitcast.55, f32[64,1024]{1,0:T(8,128)S(1)} %get-tuple-element.424.ka, f32[64,1024]{1,0:T(8,128)S(1)} %get-tuple-element.425.kb, ...), custom_call_target="tpu_custom_call" | custom-call | tf_op jit(solution)/shard_map/while/body/eval_jaxpr/pallas_call | solution.py:410
  100.9 2.7 %eval_jaxpr.11 = f32[256,128]{1,0:T(8,128)} custom-call(f32[1,1]{1,0:T(1,128)} %get-tuple-element.435.v1_ref, f32[64,1024]{1,0:T(8,128)S(1)} %get-tuple-element.433.rows_ref, f32[24,1024]{1,0:T(8,128)S(1)} %get-tuple-element.436.tab_ref, f32[16,64]{1,0:T(8,128)S(1)} %get-tuple-element.387.coll_ref), custom_call_target="tpu_custom_call" | custom-call | tf_op jit(solution)/shard_map/while/body/eval_jaxpr/pallas_call | solution.py:410
  103.6 4.0 %all-to-all-start.3 = ((f32[32,8,128]{2,1,0:T(8,128)}), f32[32,8,128]{2,1,0:T(8,128)S(1)}, u32[]{:S(2)}, u32[]{:S(2)}) async-start(f32[32,8,128]{2,1,0:T(8,128)} %bitcast.52), calls=%async_computation.3 | async-start | bytes 262144 | tf_op jit(solution)/shard_map/while/body/eval_jaxpr/all_to_all | solution.py:426
  108.0 7.3 %all-to-all-done.3 = f32[32,8,128]{2,1,0:T(8,128)S(1)} async-done(((f32[32,8,128]{2,1,0:T(8,128)}), f32[32,8,128]{2,1,0:T(8,128)S(1)}, u32[]{:S(2)}, u32[]{:S(2)}) %all-to-all-start.3) | async-done | bytes 131104 | tf_op jit(solution)/shard_map/while/body/eval_jaxpr/all_to_all | solution.py:426
  115.3 9.2 %all_to_all.60 = f32[8,8,128]{2,1,0:T(8,128)S(1)} all-to-all(f32[8,8,128]{2,1,0:T(8,128)S(1)} %broadcast_in_dim.50), channel_id=1, replica_groups=mesh['bx'=4,'by'=8,'bz'=8] {'bz'}, dimensions={0} | all-to-all | bytes 65536 | tf_op jit(solution)/shard_map/while/body/eval_jaxpr/all_to_all | solution.py:426
  125.2 5.1 %all-to-all-start.5 = ((f32[32,8,128]{2,1,0:T(8,128)}), f32[32,8,128]{2,1,0:T(8,128)S(1)}, u32[]{:S(2)}, u32[]{:S(2)}) async-start(f32[32,8,128]{2,1,0:T(8,128)} %broadcast_in_dim.51), calls=%async_computation.5 | async-start | bytes 262144 | tf_op jit(solution)/shard_map/while/body/eval_jaxpr/all_to_all | solution.py:426
  130.4 3.6 %collective-permute-start.4 = (f32[64,256]{1,0:T(8,128)S(1)}, f32[64,256]{1,0:T(8,128)S(1)}, u32[]{:S(2)}, u32[]{:S(2)}) collective-permute-start(f32[64,256]{1,0:T(8,128)S(1)} %get-tuple-element.377.yh), channel_id=1, source_target_pairs={{0,56},{8,0},{16,8},{24,16},{32,24},{40,32},{48,40},{56,48},{1,57}... | collective-permute-start | bytes 196616 | tf_op jit(solution)/shard_map/while/body/eval_jaxpr/ppermute | solution.py:486
  134.1 2.9 %collective-permute-done.5 = f32[64,128]{1,0:T(8,128)S(1)} collective-permute-done((f32[64,128]{1,0:T(8,128)S(1)}, f32[64,128]{1,0:T(8,128)S(1)}, u32[]{:S(2)}, u32[]{:S(2)}) %collective-permute-start.5) | collective-permute-done | bytes 32800 | tf_op jit(solution)/shard_map/while/body/eval_jaxpr/ppermute | solution.py:487
  137.0 1.0 all-to-all-done.5
  138.0 5.4 %eval_jaxpr.6 = (f32[64,1024]{1,0:T(8,128)S(1)}, f32[64,464]{1,0:T(8,128)S(1)}, f32[32,64]{1,0:T(8,128)S(1)}, f32[32,64]{1,0:T(8,128)S(1)}, f32[64,384]{1,0:T(8,...) custom-call(f32[256,128]{1,0:T(8,128)S(1)} %get-tuple-element.415.su, ...), custom_call_target="tpu_custom_call" | custom-call | tf_op jit(solution)/shard_map/while/body/eval_jaxpr/pallas_call | solution.py:410
  143.4 2.9 %collective-permute-start = (f32[64,1024]{1,0:T(8,128)S(1)}, f32[64,1024]{1,0:T(8,128)S(1)}, u32[]{:S(2)}, u32[]{:S(2)}) collective-permute-start(f32[64,1024]{1,0:T(8,128)S(1)} %get-tuple-element.425.kb), channel_id=1, source_target_pairs={{0,64},{64,128},{128,192},{192,0},{1,65},{65,129},{129,193},{193,1... | collective-permute-start | bytes 786440 | tf_op jit(solution)/shard_map/while/body/eval_jaxpr/ppermute | solution.py:478
  146.4 1.3 eval_jaxpr.7
  148.1 2.8 %eval_jaxpr.8.part_ref = f32[272,64]{1,0:T(8,128)S(1)} custom-call(f32[32,64]{1,0:T(8,128)S(1)} %get-tuple-element.379.seln_ref, f32[64,1024]{1,0:T(8,128)S(1)} %get-tuple-element.424.ka, f32[64,1024]{1,0:T(8,128)S(1)} %get-tuple-element.425.kb), custom_call_target="tpu_custom_call" | custom-call | tf_op jit(solution)/shard_map/while/body/eval_jaxpr/pallas_call | solution.py:410
  151.8 1.2 collective-permute-done.1.yl
  153.5 12.0 %all_to_all.58 = f32[32,4,128]{2,1,0:T(4,128)S(1)} all-to-all(f32[32,4,128]{2,1,0:T(4,128)S(1)} %bitcast.54), channel_id=1, replica_groups=mesh['bx'=4,'by'=8,'bz'=8] {'bx','by'}, dimensions={0} | all-to-all | bytes 131072 | tf_op jit(solution)/shard_map/while/body/eval_jaxpr/all_to_all | solution.py:426
  165.6 9.0 %all_to_all.59 = f32[8,4,128]{2,1,0:T(4,128)S(1)} all-to-all(f32[8,4,128]{2,1,0:T(4,128)S(1)} %broadcast_in_dim.48), channel_id=1, replica_groups=mesh['bx'=4,'by'=8,'bz'=8] {'bz'}, dimensions={0} | all-to-all | bytes 32768 | tf_op jit(solution)/shard_map/while/body/eval_jaxpr/all_to_all | solution.py:426
  175.2 5.1 %all-to-all-start.2 = ((f32[32,4,128]{2,1,0:T(4,128)}), f32[32,4,128]{2,1,0:T(4,128)S(1)}, u32[]{:S(2)}, u32[]{:S(2)}) async-start(f32[32,4,128]{2,1,0:T(4,128)} %broadcast_in_dim.49), calls=%async_computation.2 | async-start | bytes 131072 | tf_op jit(solution)/shard_map/while/body/eval_jaxpr/all_to_all | solution.py:426
  180.4 7.3 %all-to-all-done.2 = f32[32,4,128]{2,1,0:T(4,128)S(1)} async-done(((f32[32,4,128]{2,1,0:T(4,128)}), f32[32,4,128]{2,1,0:T(4,128)S(1)}, u32[]{:S(2)}, u32[]{:S(2)}) %all-to-all-start.2) | async-done | bytes 65568 | tf_op jit(solution)/shard_map/while/body/eval_jaxpr/all_to_all | solution.py:426
  187.7 6.9 %eval_jaxpr.10 = (f32[16,64]{1,0:T(8,128)S(1)}, f32[64,1024]{1,0:T(8,128)S(1)}, f32[64,64]{1,0:T(8,128)S(1)}) custom-call(f32[1,1]{1,0:T(1,128)} %get-tuple-element.435.v1_ref, f32[128,128]{1,0:T(8,128)S(1)} %bitcast.55, f32[64,1024]{1,0:T(8,128)S(1)} %get-tuple-element.424.ka, f32[64,1024]{1,0:T(8,128)S(1)} %get-tuple-element.425.kb, ...), custom_call_target="tpu_custom_call" | custom-call | tf_op jit(solution)/shard_map/while/body/eval_jaxpr/pallas_call | solution.py:410
  194.6 2.7 %eval_jaxpr.11 = f32[256,128]{1,0:T(8,128)} custom-call(f32[1,1]{1,0:T(1,128)} %get-tuple-element.435.v1_ref, f32[64,1024]{1,0:T(8,128)S(1)} %get-tuple-element.433.rows_ref, f32[24,1024]{1,0:T(8,128)S(1)} %get-tuple-element.436.tab_ref, f32[16,64]{1,0:T(8,128)S(1)} %get-tuple-element.387.coll_ref), custom_call_target="tpu_custom_call" | custom-call | tf_op jit(solution)/shard_map/while/body/eval_jaxpr/pallas_call | solution.py:410
  197.3 4.0 %all-to-all-start.3 = ((f32[32,8,128]{2,1,0:T(8,128)}), f32[32,8,128]{2,1,0:T(8,128)S(1)}, u32[]{:S(2)}, u32[]{:S(2)}) async-start(f32[32,8,128]{2,1,0:T(8,128)} %bitcast.52), calls=%async_computation.3 | async-start | bytes 262144 | tf_op jit(solution)/shard_map/while/body/eval_jaxpr/all_to_all | solution.py:426
  201.7 7.3 %all-to-all-done.3 = f32[32,8,128]{2,1,0:T(8,128)S(1)} async-done(((f32[32,8,128]{2,1,0:T(8,128)}), f32[32,8,128]{2,1,0:T(8,128)S(1)}, u32[]{:S(2)}, u32[]{:S(2)}) %all-to-all-start.3) | async-done | bytes 131104 | tf_op jit(solution)/shard_map/while/body/eval_jaxpr/all_to_all | solution.py:426
  209.0 9.2 %all_to_all.60 = f32[8,8,128]{2,1,0:T(8,128)S(1)} all-to-all(f32[8,8,128]{2,1,0:T(8,128)S(1)} %broadcast_in_dim.50), channel_id=1, replica_groups=mesh['bx'=4,'by'=8,'bz'=8] {'bz'}, dimensions={0} | all-to-all | bytes 65536 | tf_op jit(solution)/shard_map/while/body/eval_jaxpr/all_to_all | solution.py:426
  218.9 5.1 %all-to-all-start.5 = ((f32[32,8,128]{2,1,0:T(8,128)}), f32[32,8,128]{2,1,0:T(8,128)S(1)}, u32[]{:S(2)}, u32[]{:S(2)}) async-start(f32[32,8,128]{2,1,0:T(8,128)} %broadcast_in_dim.51), calls=%async_computation.5 | async-start | bytes 262144 | tf_op jit(solution)/shard_map/while/body/eval_jaxpr/all_to_all | solution.py:426
  224.0 3.6 %collective-permute-start.4 = (f32[64,256]{1,0:T(8,128)S(1)}, f32[64,256]{1,0:T(8,128)S(1)}, u32[]{:S(2)}, u32[]{:S(2)}) collective-permute-start(f32[64,256]{1,0:T(8,128)S(1)} %get-tuple-element.377.yh), channel_id=1, source_target_pairs={{0,56},{8,0},{16,8},{24,16},{32,24},{40,32},{48,40},{56,48},{1,57}... | collective-permute-start | bytes 196616 | tf_op jit(solution)/shard_map/while/body/eval_jaxpr/ppermute | solution.py:486
  227.8 2.9 %collective-permute-done.5 = f32[64,128]{1,0:T(8,128)S(1)} collective-permute-done((f32[64,128]{1,0:T(8,128)S(1)}, f32[64,128]{1,0:T(8,128)S(1)}, u32[]{:S(2)}, u32[]{:S(2)}) %collective-permute-start.5) | collective-permute-done | bytes 32800 | tf_op jit(solution)/shard_map/while/body/eval_jaxpr/ppermute | solution.py:487
  232.5 4.6 %shard_map.69 = (f32[64,64]{1,0:T(8,128)}, f32[64,1024]{1,0:T(8,128)}) custom-call(f32[256,128]{1,0:T(8,128)S(1)} %get-tuple-element.107.sums_ref, f32[64,64]{1,0:T(8,128)S(1)} %get-tuple-element.104.cxi_ref, f32[64,1024]{1,0:T(8,128)S(1)} %get-tuple-element.108.rows_ref, f32[24,1024]{1,0:T(8,128)S(1)} %get-tuple-element.450, f32[160,16]{1,0:T(8,128)S(1)} %get-tuple-element.454), custom_call_target="tpu_custom_call" | custom-call | tf_op jit(solution)/shard_map/pallas_call | solution.py:410
  (79 shorter events, 12.6 us)
Async XLA Ops:
  0.6 1.1 copy-start.1
  2.1 39.4 %collective-permute-start.7 = (f32[64,256]{1,0:T(8,128)S(1)}, f32[64,256]{1,0:T(8,128)S(1)}, u32[]{:S(2)}, u32[]{:S(2)}) collective-permute-start(f32[64,256]{1,0:T(8,128)S(1)} %bitcast.69), channel_id=1, source_target_pairs={{0,8},{8,16},{16,24},{24,32},{32,40},{40,48},{48,56},{56,0},{1,9},... | collective-permute-start | bytes 196616 | tf_op jit(solution)/shard_map/ppermute | solution.py:479
  7.1 15.3 %all-to-all-start.6 = ((f32[32,8,128]{2,1,0:T(8,128)}), f32[32,8,128]{2,1,0:T(8,128)S(1)}, u32[]{:S(2)}, u32[]{:S(2)}) async-start(f32[32,8,128]{2,1,0:T(8,128)} %bitcast.3), calls=%async_computation.6 | async-start | bytes 262144 | tf_op jit(solution)/shard_map/all_to_all | solution.py:426
  14.9 26.6 %collective-permute-start.9 = (f32[64,1024]{1,0:T(8,128)S(1)}, f32[64,1024]{1,0:T(8,128)S(1)}, u32[]{:S(2)}, u32[]{:S(2)}) collective-permute-start(f32[64,1024]{1,0:T(8,128)S(1)} %bitcast.56), channel_id=1, source_target_pairs={{0,192},{64,0},{128,64},{192,128},{1,193},{65,1},{129,65},{193,129... | collective-permute-start | bytes 786440 | tf_op jit(solution)/shard_map/ppermute | solution.py:485
  15.3 26.3 %collective-permute-start.6 = (f32[64,1024]{1,0:T(8,128)S(1)}, f32[64,1024]{1,0:T(8,128)S(1)}, u32[]{:S(2)}, u32[]{:S(2)}) collective-permute-start(f32[64,1024]{1,0:T(8,128)S(1)} %bitcast.58), channel_id=1, source_target_pairs={{0,64},{64,128},{128,192},{192,0},{1,65},{65,129},{129,193},{193,1... | collective-permute-start | bytes 786440 | tf_op jit(solution)/shard_map/ppermute | solution.py:478
  23.1 18.4 %all-to-all-start.7 = ((f32[32,8,128]{2,1,0:T(8,128)}), f32[32,8,128]{2,1,0:T(8,128)S(1)}, u32[]{:S(2)}, u32[]{:S(2)}) async-start(f32[32,8,128]{2,1,0:T(8,128)} %broadcast_in_dim.13), calls=%async_computation.7 | async-start | bytes 262144 | tf_op jit(solution)/shard_map/all_to_all | solution.py:426
  27.6 9.4 %collective-permute-start.11 = (f32[64,128]{0,1:T(8,128)S(1)}, f32[64,128]{0,1:T(8,128)S(1)}, u32[]{:S(2)}, u32[]{:S(2)}) collective-permute-start(f32[64,128]{0,1:T(8,128)S(1)} %concatenate.7), channel_id=1, source_target_pairs={{0,7},{1,0},{2,1},{3,2},{4,3},{5,4},{6,5},{7,6},{8,15},{9,8},{10,9... | collective-permute-start | bytes 98312 | tf_op jit(solution)/shard_map/ppermute | solution.py:487
  33.2 8.3 %collective-permute-start.10 = (f32[64,256]{1,0:T(8,128)S(1)}, f32[64,256]{1,0:T(8,128)S(1)}, u32[]{:S(2)}, u32[]{:S(2)}) collective-permute-start(f32[64,256]{1,0:T(8,128)S(1)} %bitcast.70), channel_id=1, source_target_pairs={{0,56},{8,0},{16,8},{24,16},{32,24},{40,32},{48,40},{56,48},{1,57}... | collective-permute-start | bytes 196616 | tf_op jit(solution)/shard_map/ppermute | solution.py:486
  37.0 0.8 copy-start.2
  37.0 4.4 %collective-permute-start.8 = (f32[64,128]{0,1:T(8,128)S(1)}, f32[64,128]{0,1:T(8,128)S(1)}, u32[]{:S(2)}, u32[]{:S(2)}) collective-permute-start(f32[64,128]{0,1:T(8,128)S(1)} %concatenate.6), channel_id=1, source_target_pairs={{0,1},{1,2},{2,3},{3,4},{4,5},{5,6},{6,7},{7,0},{8,9},{9,10},{10,1... | collective-permute-start | bytes 98312 | tf_op jit(solution)/shard_map/ppermute | solution.py:480
  37.8 3.7 %copy-start = (f32[160,16]{1,0:T(8,128)S(1)}, f32[160,16]{1,0:T(8,128)}, u32[]{:S(2)}) copy-start(f32[160,16]{1,0:T(8,128)} %constant.53.clone.cons_ref) | copy-start | bytes 30724
  47.2 11.1 %collective-permute-start = (f32[64,1024]{1,0:T(8,128)S(1)}, f32[64,1024]{1,0:T(8,128)S(1)}, u32[]{:S(2)}, u32[]{:S(2)}) collective-permute-start(f32[64,1024]{1,0:T(8,128)S(1)} %get-tuple-element.425.kb), channel_id=1, source_target_pairs={{0,64},{64,128},{128,192},{192,0},{1,65},{65,129},{129,193},{193,1... | collective-permute-start | bytes 786440 | tf_op jit(solution)/shard_map/while/body/eval_jaxpr/ppermute | solution.py:478
  53.0 5.3 %collective-permute-start.1 = (f32[64,256]{1,0:T(8,128)S(1)}, f32[64,256]{1,0:T(8,128)S(1)}, u32[]{:S(2)}, u32[]{:S(2)}) collective-permute-start(f32[64,256]{1,0:T(8,128)S(1)} %get-tuple-element.375), channel_id=1, source_target_pairs={{0,8},{8,16},{16,24},{24,32},{32,40},{40,48},{48,56},{56,0},{1,9},... | collective-permute-start | bytes 196616 | tf_op jit(solution)/shard_map/while/body/eval_jaxpr/ppermute | solution.py:479
  53.1 4.1 %collective-permute-start.2 = (f32[64,128]{1,0:T(8,128)S(1)}, f32[64,128]{1,0:T(8,128)S(1)}, u32[]{:S(2)}, u32[]{:S(2)}) collective-permute-start(f32[64,128]{1,0:T(8,128)S(1)} %get-tuple-element.376), channel_id=1, source_target_pairs={{0,1},{1,2},{2,3},{3,4},{4,5},{5,6},{6,7},{7,0},{8,9},{9,10},{10,1... | collective-permute-start | bytes 98312 | tf_op jit(solution)/shard_map/while/body/eval_jaxpr/ppermute | solution.py:480
  81.3 12.7 %all-to-all-start.2 = ((f32[32,4,128]{2,1,0:T(4,128)}), f32[32,4,128]{2,1,0:T(4,128)S(1)}, u32[]{:S(2)}, u32[]{:S(2)}) async-start(f32[32,4,128]{2,1,0:T(4,128)} %broadcast_in_dim.49), calls=%async_computation.2 | async-start | bytes 131072 | tf_op jit(solution)/shard_map/while/body/eval_jaxpr/all_to_all | solution.py:426
  103.6 11.6 %all-to-all-start.3 = ((f32[32,8,128]{2,1,0:T(8,128)}), f32[32,8,128]{2,1,0:T(8,128)S(1)}, u32[]{:S(2)}, u32[]{:S(2)}) async-start(f32[32,8,128]{2,1,0:T(8,128)} %bitcast.52), calls=%async_computation.3 | async-start | bytes 262144 | tf_op jit(solution)/shard_map/while/body/eval_jaxpr/all_to_all | solution.py:426
  107.6 29.4 %collective-permute-start.3 = (f32[64,1024]{1,0:T(8,128)S(1)}, f32[64,1024]{1,0:T(8,128)S(1)}, u32[]{:S(2)}, u32[]{:S(2)}) collective-permute-start(f32[64,1024]{1,0:T(8,128)S(1)} %get-tuple-element.424.ka), channel_id=1, source_target_pairs={{0,192},{64,0},{128,64},{192,128},{1,193},{65,1},{129,65},{193,129... | collective-permute-start | bytes 786440 | tf_op jit(solution)/shard_map/while/body/eval_jaxpr/ppermute | solution.py:485
  125.2 12.8 %all-to-all-start.5 = ((f32[32,8,128]{2,1,0:T(8,128)}), f32[32,8,128]{2,1,0:T(8,128)S(1)}, u32[]{:S(2)}, u32[]{:S(2)}) async-start(f32[32,8,128]{2,1,0:T(8,128)} %broadcast_in_dim.51), calls=%async_computation.5 | async-start | bytes 262144 | tf_op jit(solution)/shard_map/while/body/eval_jaxpr/all_to_all | solution.py:426
  130.4 6.6 %collective-permute-start.4 = (f32[64,256]{1,0:T(8,128)S(1)}, f32[64,256]{1,0:T(8,128)S(1)}, u32[]{:S(2)}, u32[]{:S(2)}) collective-permute-start(f32[64,256]{1,0:T(8,128)S(1)} %get-tuple-element.377.yh), channel_id=1, source_target_pairs={{0,56},{8,0},{16,8},{24,16},{32,24},{40,32},{48,40},{56,48},{1,57}... | collective-permute-start | bytes 196616 | tf_op jit(solution)/shard_map/while/body/eval_jaxpr/ppermute | solution.py:486
  133.9 3.1 %collective-permute-start.5 = (f32[64,128]{1,0:T(8,128)S(1)}, f32[64,128]{1,0:T(8,128)S(1)}, u32[]{:S(2)}, u32[]{:S(2)}) collective-permute-start(f32[64,128]{1,0:T(8,128)S(1)} %get-tuple-element.378.zh), channel_id=1, source_target_pairs={{0,7},{1,0},{2,1},{3,2},{4,3},{5,4},{6,5},{7,6},{8,15},{9,8},{10,9... | collective-permute-start | bytes 98312 | tf_op jit(solution)/shard_map/while/body/eval_jaxpr/ppermute | solution.py:487
  143.4 9.6 %collective-permute-start = (f32[64,1024]{1,0:T(8,128)S(1)}, f32[64,1024]{1,0:T(8,128)S(1)}, u32[]{:S(2)}, u32[]{:S(2)}) collective-permute-start(f32[64,1024]{1,0:T(8,128)S(1)} %get-tuple-element.425.kb), channel_id=1, source_target_pairs={{0,64},{64,128},{128,192},{192,0},{1,65},{65,129},{129,193},{193,1... | collective-permute-start | bytes 786440 | tf_op jit(solution)/shard_map/while/body/eval_jaxpr/ppermute | solution.py:478
  147.7 5.3 %collective-permute-start.1 = (f32[64,256]{1,0:T(8,128)S(1)}, f32[64,256]{1,0:T(8,128)S(1)}, u32[]{:S(2)}, u32[]{:S(2)}) collective-permute-start(f32[64,256]{1,0:T(8,128)S(1)} %get-tuple-element.375), channel_id=1, source_target_pairs={{0,8},{8,16},{16,24},{24,32},{32,40},{40,48},{48,56},{56,0},{1,9},... | collective-permute-start | bytes 196616 | tf_op jit(solution)/shard_map/while/body/eval_jaxpr/ppermute | solution.py:479
  147.8 4.1 %collective-permute-start.2 = (f32[64,128]{1,0:T(8,128)S(1)}, f32[64,128]{1,0:T(8,128)S(1)}, u32[]{:S(2)}, u32[]{:S(2)}) collective-permute-start(f32[64,128]{1,0:T(8,128)S(1)} %get-tuple-element.376), channel_id=1, source_target_pairs={{0,1},{1,2},{2,3},{3,4},{4,5},{5,6},{6,7},{7,0},{8,9},{9,10},{10,1... | collective-permute-start | bytes 98312 | tf_op jit(solution)/shard_map/while/body/eval_jaxpr/ppermute | solution.py:480
  175.2 12.4 %all-to-all-start.2 = ((f32[32,4,128]{2,1,0:T(4,128)}), f32[32,4,128]{2,1,0:T(4,128)S(1)}, u32[]{:S(2)}, u32[]{:S(2)}) async-start(f32[32,4,128]{2,1,0:T(4,128)} %broadcast_in_dim.49), calls=%async_computation.2 | async-start | bytes 131072 | tf_op jit(solution)/shard_map/while/body/eval_jaxpr/all_to_all | solution.py:426
  197.3 11.6 %all-to-all-start.3 = ((f32[32,8,128]{2,1,0:T(8,128)}), f32[32,8,128]{2,1,0:T(8,128)S(1)}, u32[]{:S(2)}, u32[]{:S(2)}) async-start(f32[32,8,128]{2,1,0:T(8,128)} %bitcast.52), calls=%async_computation.3 | async-start | bytes 262144 | tf_op jit(solution)/shard_map/while/body/eval_jaxpr/all_to_all | solution.py:426
  201.3 29.4 %collective-permute-start.3 = (f32[64,1024]{1,0:T(8,128)S(1)}, f32[64,1024]{1,0:T(8,128)S(1)}, u32[]{:S(2)}, u32[]{:S(2)}) collective-permute-start(f32[64,1024]{1,0:T(8,128)S(1)} %get-tuple-element.424.ka), channel_id=1, source_target_pairs={{0,192},{64,0},{128,64},{192,128},{1,193},{65,1},{129,65},{193,129... | collective-permute-start | bytes 786440 | tf_op jit(solution)/shard_map/while/body/eval_jaxpr/ppermute | solution.py:485
  218.9 12.8 %all-to-all-start.5 = ((f32[32,8,128]{2,1,0:T(8,128)}), f32[32,8,128]{2,1,0:T(8,128)S(1)}, u32[]{:S(2)}, u32[]{:S(2)}) async-start(f32[32,8,128]{2,1,0:T(8,128)} %broadcast_in_dim.51), calls=%async_computation.5 | async-start | bytes 262144 | tf_op jit(solution)/shard_map/while/body/eval_jaxpr/all_to_all | solution.py:426
  224.0 6.6 %collective-permute-start.4 = (f32[64,256]{1,0:T(8,128)S(1)}, f32[64,256]{1,0:T(8,128)S(1)}, u32[]{:S(2)}, u32[]{:S(2)}) collective-permute-start(f32[64,256]{1,0:T(8,128)S(1)} %get-tuple-element.377.yh), channel_id=1, source_target_pairs={{0,56},{8,0},{16,8},{24,16},{32,24},{40,32},{48,40},{56,48},{1,57}... | collective-permute-start | bytes 196616 | tf_op jit(solution)/shard_map/while/body/eval_jaxpr/ppermute | solution.py:486
  227.6 3.1 %collective-permute-start.5 = (f32[64,128]{1,0:T(8,128)S(1)}, f32[64,128]{1,0:T(8,128)S(1)}, u32[]{:S(2)}, u32[]{:S(2)}) collective-permute-start(f32[64,128]{1,0:T(8,128)S(1)} %get-tuple-element.378.zh), channel_id=1, source_target_pairs={{0,7},{1,0},{2,1},{3,2},{4,3},{5,4},{6,5},{7,6},{8,15},{9,8},{10,9... | collective-permute-start | bytes 98312 | tf_op jit(solution)/shard_map/while/body/eval_jaxpr/ppermute | solution.py:487
where the time goes:
time: 239 us; the launch traced here: 238 us
  starting transfers between devices  71.3 us (30%)
  blocking collectives  61.2 us (26%)
  waiting for transfers between devices  48.7 us (20%)
  Pallas kernels  46.9 us (20%)
  local copies, waits for them, and re-layouts  6.81 us (3%)
    all_to_all x6, blocking collectives, swap(): return lax.all_to_all(chunks, axis, 0, 0, tiled=True)  61.2 us
    pallas_call x15, Pallas kernels, call(): pl.pallas_call(kernel, out_shape=shapes, in_specs=specs, out_specs=[pl.Bl...  46.9 us
    all_to_all x8, starting transfers between devices, swap(): return lax.all_to_all(chunks, axis, 0, 0, tiled=True)  40.4 us
    all_to_all x8, waiting for transfers between devices, swap(): return lax.all_to_all(chunks, axis, 0, 0, tiled=True)  35.1 us
    ppermute x3, starting transfers between devices, high_halo(): lax.ppermute(yh, 'by', route('by', -1))  10.7 us
    ppermute x3, starting transfers between devices, low_halo(): lax.ppermute(xl, 'bx', route('bx', 1))  10.5 us
    ppermute x3, starting transfers between devices, high_halo(): lax.ppermute(zh, 'bz', route('bz', -1))  5.85 us
    ppermute x3, waiting for transfers between devices, high_halo(): lax.ppermute(zh, 'bz', route('bz', -1))  5.77 us
  transfers between devices with their start and end apart: 26, of which 14 were waited for; matrix products, arithmetic and copies ran while one was open for 1% of the time, Pallas kernels for 5%

commit v1 on v0

--- a/solution.py
+++ b/solution.py
@@ -7,6 +7,7 @@
 from jax.experimental import pallas as pl
 from jax.experimental.pallas import tpu as pltpu
 from jax.sharding import PartitionSpec as P
+
 
 VEL_N = 32
 STEPS = 2
@@ -148,12 +149,45 @@
     return jnp.where(iota((RANK, RANK), 0) <= iota((RANK, RANK), 1), plus, minus)
 
 
-def tables_kernel(v1_ref, tab_ref):
+def weighted_payload(rows, v1, tab_ref, out_ref, stack_ref, scale, collide):
+    modes = tab_ref[0:16, :]
+    v2, v3 = tab_ref[18:19, :], tab_ref[19:20, :]
+    weights = [None, jnp.maximum(v2, 0.0), jnp.minimum(v2, 0.0)]
+    weights += [jnp.maximum(v3, 0.0), jnp.minimum(v3, 0.0)]
+    for i in range(5):
+        w = weights[i]
+        stack_ref[80 * i : 80 * i + 64, :] = rows if w is None else rows * w
+        stack_ref[80 * i + 64 : 80 * i + 80, :] = modes if w is None else modes * w
+    stack_ref[400:408, :] = tab_ref[16:24, :]
+    res = mmt(stack_ref[...], rows) * scale
+    quads = [res[80 * i : 80 * i + 64] for i in range(5)]
+    cross = [res[80 * i + 64 : 80 * i + 80] for i in range(5)]
+    out_ref[...] = jnp.zeros_like(out_ref)
+    out_ref[0:64, 0:64] = quads[0]
+    out_ref[128:144, 0:64] = cross[0]
+    if collide is not None:
+        out_ref[136:152, 64:128] = collide
+    v1p, v1m = jnp.maximum(v1, 0.0), jnp.minimum(v1, 0.0)
+    pairs = [(quads[0] * v1p, quads[0] * v1m), (quads[1], quads[2]), (quads[3], quads[4])]
+    crosses = [cross[0] * v1p, cross[0] * v1m] + cross[1:]
+    out_ref[0:64, 64:128] = pair_block(*pairs[1])
+    out_ref[64:128, 0:64] = pair_block(*pairs[0])
+    out_ref[64:128, 64:128] = pair_block(*pairs[2])
+    for i in range(6):
+        out_ref[144 + 16 * i : 160 + 16 * i, 0:64] = crosses[i]
+    out_ref[128:136, 64:128] = res[400:408]
+    for d in range(3):
+        diag = jnp.sum(pairs[d][1] * eye(), axis=0, keepdims=True)
+        out_ref[152 + d : 153 + d, 64:128] = diag
+
+
+def start_kernel(v1_ref, rows_ref, out_ref, tab_ref, stack_ref):
+    v1 = v1_ref[0, 0]
     lanes = tab_ref.shape[1]
     at = iota((1, lanes), 1)
     v2 = SPEED_MAX * (2.0 * (at // VEL_N).astype(F32) + 1.0 - VEL_N) / VEL_N
     v3 = SPEED_MAX * (2.0 * (at % VEL_N).astype(F32) + 1.0 - VEL_N) / VEL_N
-    v1 = jnp.full((1, lanes), v1_ref[0, 0], F32)
+    v1 = jnp.full((1, lanes), v1, F32)
     w = jnp.exp(-0.5 * (v1 * v1 + v2 * v2 + v3 * v3)) / (line_mean() ** 3)
     tab_ref[...] = jnp.zeros_like(tab_ref)
     modes = [w, w * v1, w * v2, w * v3]
@@ -163,45 +197,7 @@
         tab_ref[i : i + 1, :] = m
     for i, m in enumerate([jnp.ones_like(v1), v1, v2, v3]):
         tab_ref[16 + i : 17 + i, :] = m
-
-
-def weigh_kernel(scale, v1_ref, rows_ref, tab_ref, coll_ref, out_ref, stack_ref, res_ref):
-    v1 = v1_ref[0, 0]
-    lanes = rows_ref.shape[1]
-    width = lanes // 4
-    res_ref[...] = jnp.zeros_like(res_ref)
-
-    def chunk(c, carry):
-        cols = pl.ds(pl.multiple_of(c * width, width), width)
-        rows, modes = rows_ref[:, cols], tab_ref[0:16, cols]
-        v2, v3 = tab_ref[18:19, cols], tab_ref[19:20, cols]
-        weights = [None, jnp.maximum(v2, 0.0), jnp.minimum(v2, 0.0)]
-        weights += [jnp.maximum(v3, 0.0), jnp.minimum(v3, 0.0)]
-        for i, w in enumerate(weights):
-            stack_ref[80 * i : 80 * i + 64, :] = rows if w is None else rows * w
-            stack_ref[80 * i + 64 : 80 * i + 80, :] = modes if w is None else modes * w
-        stack_ref[400:408, :] = tab_ref[16:24, cols]
-        res_ref[...] += mmt(stack_ref[...], rows)
-        return carry
-
-    lax.fori_loop(0, 4, chunk, 0)
-    quads = [res_ref[80 * i : 80 * i + 64, :] * scale for i in range(5)]
-    cross = [res_ref[80 * i + 64 : 80 * i + 80, :] * scale for i in range(5)]
-    out_ref[...] = jnp.zeros_like(out_ref)
-    out_ref[0:64, 0:64] = quads[0]
-    out_ref[128:144, 0:64] = cross[0]
-    v1p, v1m = jnp.maximum(v1, 0.0), jnp.minimum(v1, 0.0)
-    pairs = [(quads[0] * v1p, quads[0] * v1m), (quads[1], quads[2]), (quads[3], quads[4])]
-    crosses = [cross[0] * v1p, cross[0] * v1m] + cross[1:]
-    out_ref[0:64, 64:128] = pair_block(*pairs[1])
-    out_ref[64:128, 0:64] = pair_block(*pairs[0])
-    out_ref[64:128, 64:128] = pair_block(*pairs[2])
-    for i in range(6):
-        out_ref[144 + 16 * i : 160 + 16 * i, 0:64] = crosses[i]
-    out_ref[128:136, 64:128] = res_ref[400:408, :] * scale
-    out_ref[136:152, 64:128] = coll_ref[...]
-    for d in range(3):
-        out_ref[152 + d : 153 + d, 64:128] = jnp.sum(pairs[d][1] * eye(), axis=0, keepdims=True)
+    weighted_payload(rows_ref[...], v1_ref[0, 0], tab_ref, out_ref, stack_ref, 1.0, None)
 
 
 def symmetric(sums, gain, cons):
@@ -327,15 +323,7 @@
         stack_ref[256:272, at : at + n] = features(seln_ref[...], field)
     stack_ref[64:128, 0:n] = jnp.zeros((RANK, n), F32)
     stack_ref[64:128, n : 2 * n] = ka[...]
-    out_ref[...] = jnp.zeros_like(out_ref)
-    width = n // 2
-
-    def chunk(c, carry):
-        cols = pl.ds(pl.multiple_of(c * width, width), width)
-        out_ref[...] += mmt(stack_ref[:, cols], stack_ref[0:64, cols])
-        return carry
-
-    lax.fori_loop(0, 4, chunk, 0)
+    out_ref[...] = mmt(stack_ref[...], stack_ref[0:64, :])
 
 
 def edge_kernel(part_ref, ka, xl, yl, yh, zl, zh, out_ref):
@@ -349,8 +337,8 @@
 
 
 def core_kernel(
-    count, cells, v1_ref, sums_ref, ka, kb, rows_ref, gain_ref, tab_ref, cons_ref,
-    gw_ref, mode_ref, mom_ref, civ_ref, ginv_ref, coll_ref, rows_out, cxi_ref, base_ref,
+    count, cells, nz, v1_ref, sums_ref, ka, kb, rows_ref, gain_ref, tab_ref, cons_ref,
+    gw_ref, mode_ref, mom_ref, civ_ref, ginv_ref, out_ref, rows_out, cxi_ref, stack_ref, base_ref,
 ):
     v1 = v1_ref[0, 0]
     rows = rows_ref[...] + mm(gain_ref[...], tab_ref[0:16, :])
@@ -388,8 +376,16 @@
     move += [-TIME_STEP * m for m in (lower[1], upper[1], lower[2], upper[2])]
     move = mm(jnp.concatenate(move, axis=0), y)
     move = jnp.concatenate([move[64 * t : 64 * t + 64] for t in range(5)], axis=1)
-    rows_out[...] = mm(move, base_ref[...])
-    coll_ref[...] = collide
+    rows = mm(move, base_ref[...])
+    rows_out[...] = rows
+    weighted_payload(rows, v1, tab_ref, out_ref, stack_ref, 1.0 / nz, collide)
+
+
+def space_kernel(cxi_ref, ka, kb, out_ref):
+    for p, ref in enumerate((ka, kb)):
+        field = mm(cxi_ref[...], ref[...])
+        for y in range(out_ref.shape[2]):
+            out_ref[:, p, y, :] = field[:, 128 * y : 128 * y + 128]
 
 
 def finish_kernel(count, cells, sums_ref, cxi_ref, rows_ref, tab_ref, cons_ref, low_ref, out_ref):
@@ -458,41 +454,34 @@
 
     fa = space_factor[:, 0].reshape(RANK, half)
     fb = space_factor[:, 1].reshape(RANK, half)
-    (tab,) = call(tables_kernel, [(24, vel_rows)], [], v1)
-
-    def weigh(rows, coll, scale):
-        return call(
-            functools.partial(weigh_kernel, scale),
-            [(256, 128)], [(408, vel_rows // 4), (408, RANK)], v1, rows, tab, coll,
-        )[0]
-
-    payload = weigh(velocity_factor, jnp.zeros((16, RANK), F32), 1.0)
+    payload, tab = call(
+        start_kernel, [(256, 128), (24, vel_rows)], [(408, vel_rows)], v1, velocity_factor
+    )
     yl = space_factor[:, :, -1].reshape(RANK, 256)
     yh = space_factor[:, :, 0].reshape(RANK, 256)
     pad = jnp.zeros((RANK, 128 - 2 * shape[2]), F32)
     zl = jnp.concatenate([space_factor[:, :, :, -1].reshape(RANK, -1), pad], axis=1)
     zh = jnp.concatenate([space_factor[:, :, :, 0].reshape(RANK, -1), pad], axis=1)
 
-    def low_halo(xl, yl, zl):
-        return (
-            lax.ppermute(xl, "bx", route("bx", 1)),
-            lax.ppermute(yl, "by", route("by", 1)),
-            lax.ppermute(zl, "bz", route("bz", 1)),
-        )
-
-    def high_halo(xh, yh, zh):
-        return (
-            lax.ppermute(xh, "bx", route("bx", -1)),
-            lax.ppermute(yh, "by", route("by", -1)),
-            lax.ppermute(zh, "bz", route("bz", -1)),
-        )
+    def halo(planes, step):
+        out = []
+        for field, axis in zip(planes, ("bx", "by", "bz")):
+            out.append(lax.ppermute(field, axis, route(axis, step)))
+        return tuple(out)
+
+    def low_halo(*planes):
+        return halo(planes, 1)
+
+    def high_halo(*planes):
+        return halo(planes, -1)
 
     low = low_halo(fb, yl, zl)
     high = high_halo(fa, yh, zh)
-    sums = plane_gather(plane_sum(payload))
+    part = plane_sum(payload)
+    sums = plane_gather(part)
 
     def step(turn, carry):
-        fa, fb, low, high, sums, rows, base = carry
+        fa, fb, low, high, sums, rows, base, _ = carry
         kb, maps, sel, seln, gw, mode_rows, moments, civ, ginv, gain = call(
             functools.partial(maps_kernel, count, cells),
             [(RANK, half), (RANK, 464), (32, RANK), (32, RANK), (RANK, 384), (16, RANK), (8, RANK),
@@ -511,20 +500,18 @@
         (payload,) = call(edge_kernel, [(128, 128)], [], part, ka, low[0], low[1], yh, low[2], zh)
         high = high_halo(ka, yh, zh)
         sums = plane_gather(line_sum(plane_sum(payload)))
-        coll, rows, base = call(
-            functools.partial(core_kernel, count, cells),
-            [(16, RANK), (RANK, vel_rows), (RANK, RANK)],
-            [(320, vel_rows)],
+        payload, rows, base = call(
+            functools.partial(core_kernel, count, cells, nz),
+            [(256, 128), (RANK, vel_rows), (RANK, RANK)],
+            [(408, vel_rows), (320, vel_rows)],
             v1, sums, ka, kb, rows, gain, tab, cons, gw, mode_rows, moments, civ, ginv,
         )
-        sums = plane_gather(line_sum(plane_sum(weigh(rows, coll, 1.0 / nz))))
-        return ka, kb, low, high, sums, rows, base
-
-    carry = (fa, fb, low, high, sums, velocity_factor, core_matrix.T)
-    ka, kb, _, _, sums, rows, base = lax.fori_loop(0, STEPS, step, carry)
-    new_space = jnp.stack(
-        [mm(base, ka).reshape(RANK, *shape[2:]), mm(base, kb).reshape(RANK, *shape[2:])], axis=1
-    )
+        (space,) = call(space_kernel, [shape], [], base, ka, kb)
+        sums = plane_gather(line_sum(plane_sum(payload)))
+        return ka, kb, low, high, sums, rows, base, space
+
+    carry = (fa, fb, low, high, sums, velocity_factor, core_matrix.T, jnp.zeros(shape, F32))
+    _, _, _, _, sums, rows, base, new_space = lax.fori_loop(0, STEPS, step, carry)
     new_core, new_velocity = call(
         functools.partial(finish_kernel, count, cells),
         [(RANK, RANK), (RANK, vel_rows)], [], sums, base, rows, tab, cons,

time: 239 us -> 234 us (0.979)
    pallas_call x15 -> x14, Pallas kernels: 46.9 us -> 45.5 us  [call(): pl.pallas_call(kernel, out_shape=shapes, in_specs=specs, out_specs=[pl.Bl...]
where the time goes in v1:
time: 234 us; the launch traced here: 233 us
  starting transfers between devices  71.3 us (30%)
  blocking collectives  61.2 us (26%)
  waiting for transfers between devices  47.1 us (20%)
  Pallas kernels  45.5 us (19%)
  local copies, waits for them, and re-layouts  6.7 us (3%)
    all_to_all x6, blocking collectives, swap(): return lax.all_to_all(chunks, axis, 0, 0, tiled=True)  61.2 us
    pallas_call x14, Pallas kernels, call(): pl.pallas_call(kernel, out_shape=shapes, in_specs=specs, out_specs=[pl.Bl...  45.5 us
    all_to_all x8, starting transfers between devices, swap(): return lax.all_to_all(chunks, axis, 0, 0, tiled=True)  40.4 us
    all_to_all x8, waiting for transfers between devices, swap(): return lax.all_to_all(chunks, axis, 0, 0, tiled=True)  35.1 us
    ppermute x18, starting transfers between devices, halo(): out.append(lax.ppermute(field, axis, route(axis, step)))  30.9 us
    ppermute x18, waiting for transfers between devices, halo(): out.append(lax.ppermute(field, axis, route(axis, step)))  11.9 us
  transfers between devices with their start and end apart: 26, of which 14 were waited for; matrix products, arithmetic and copies ran while one was open for 1% of the time, Pallas kernels for 5%

profile of v1, /device:TPU:1, one launch (start us, length us, event | category | flops | bytes accessed | tf_op | source)
XLA Modules:
  0.0 233.2 jit_solution(15866414046860880004)
XLA Ops:
  0.6 1.0 copy.81.rows_ref
  2.1 2.1 collective-permute-start.7
  4.3 2.3 shard_map.67
  6.6 7.8 %all-to-all-start.6 = ((f32[32,8,128]{2,1,0:T(8,128)}), f32[32,8,128]{2,1,0:T(8,128)S(1)}, u32[]{:S(2)}, u32[]{:S(2)}) async-start(f32[32,8,128]{2,1,0:T(8,128)} %bitcast.3), calls=%async_computation.6 | async-start | bytes 262144 | tf_op jit(solution)/shard_map/all_to_all | solution.py:422
  14.8 3.1 %collective-permute-start.6 = (f32[64,1024]{1,0:T(8,128)S(1)}, f32[64,1024]{1,0:T(8,128)S(1)}, u32[]{:S(2)}, u32[]{:S(2)}) collective-permute-start(f32[64,1024]{1,0:T(8,128)S(1)} %bitcast.40), channel_id=1, source_target_pairs={{0,64},{64,128},{128,192},{192,0},{1,65},{65,129},{129,193},{193,1... | collective-permute-start | bytes 786440 | tf_op jit(solution)/shard_map/ppermute | solution.py:469
  17.9 4.0 %all-to-all-done.6 = f32[32,8,128]{2,1,0:T(8,128)S(1)} async-done(((f32[32,8,128]{2,1,0:T(8,128)}), f32[32,8,128]{2,1,0:T(8,128)S(1)}, u32[]{:S(2)}, u32[]{:S(2)}) %all-to-all-start.6) | async-done | bytes 131104 | tf_op jit(solution)/shard_map/all_to_all | solution.py:422
  22.6 4.0 %all-to-all-start.7 = ((f32[32,8,128]{2,1,0:T(8,128)}), f32[32,8,128]{2,1,0:T(8,128)S(1)}, u32[]{:S(2)}, u32[]{:S(2)}) async-start(f32[32,8,128]{2,1,0:T(8,128)} %broadcast_in_dim.12), calls=%async_computation.7 | async-start | bytes 262144 | tf_op jit(solution)/shard_map/all_to_all | solution.py:422
  27.1 5.6 %collective-permute-start.11 = (f32[64,128]{0,1:T(8,128)S(1)}, f32[64,128]{0,1:T(8,128)S(1)}, u32[]{:S(2)}, u32[]{:S(2)}) collective-permute-start(f32[64,128]{0,1:T(8,128)S(1)} %concatenate.7), channel_id=1, source_target_pairs={{0,7},{1,0},{2,1},{3,2},{4,3},{5,4},{6,5},{7,6},{8,15},{9,8},{10,9... | collective-permute-start | bytes 98312 | tf_op jit(solution)/shard_map/ppermute | solution.py:469
  32.8 3.5 %collective-permute-start.10 = (f32[64,256]{1,0:T(8,128)S(1)}, f32[64,256]{1,0:T(8,128)S(1)}, u32[]{:S(2)}, u32[]{:S(2)}) collective-permute-start(f32[64,256]{1,0:T(8,128)S(1)} %bitcast.50), channel_id=1, source_target_pairs={{0,56},{8,0},{16,8},{24,16},{32,24},{40,32},{48,40},{56,48},{1,57}... | collective-permute-start | bytes 196616 | tf_op jit(solution)/shard_map/ppermute | solution.py:469
  37.4 3.5 %collective-permute-done.8 = f32[64,128]{0,1:T(8,128)S(1)} collective-permute-done((f32[64,128]{0,1:T(8,128)S(1)}, f32[64,128]{0,1:T(8,128)S(1)}, u32[]{:S(2)}, u32[]{:S(2)}) %collective-permute-start.8) | collective-permute-done | bytes 32800 | tf_op jit(solution)/shard_map/ppermute | solution.py:469
  41.1 187.5 %while.33 = (s32[]{:T(128)}, f32[64,1024]{1,0:T(8,128)S(1)}, f32[64,1024]{1,0:T(8,128)S(1)}, f32[64,1024]{1,0:T(8,128)S(1)}, f32[64,256]{1,0:T(8,128)S(1)}, /*in...) while((s32[]{:T(128)}, f32[64,1024]{1,0:T(8,128)S(1)}, ...), condition=%wide.region_6.7_spmd.clone, body=%wide.region_1.6_spmd.sunk.clone.sunk | while | flops 58370 | bytes 6709765 | solution.py:514
  41.3 5.4 %eval_jaxpr.6 = (f32[64,1024]{1,0:T(8,128)S(1)}, f32[64,464]{1,0:T(8,128)S(1)}, f32[32,64]{1,0:T(8,128)S(1)}, f32[32,64]{1,0:T(8,128)S(1)}, f32[64,384]{1,0:T(8,...) custom-call(f32[256,128]{1,0:T(8,128)S(1)} %get-tuple-element.432.su, ...), custom_call_target="tpu_custom_call" | custom-call | tf_op jit(solution)/shard_map/while/body/eval_jaxpr/pallas_call | solution.py:406
  46.7 4.5 %collective-permute-start = (f32[64,1024]{1,0:T(8,128)S(1)}, f32[64,1024]{1,0:T(8,128)S(1)}, u32[]{:S(2)}, u32[]{:S(2)}) collective-permute-start(f32[64,1024]{1,0:T(8,128)S(1)} %get-tuple-element.443.kb), channel_id=1, source_target_pairs={{0,64},{64,128},{128,192},{192,0},{1,65},{65,129},{129,193},{193,1... | collective-permute-start | bytes 786440 | tf_op jit(solution)/shard_map/while/body/eval_jaxpr/ppermute | solution.py:469
  51.2 1.3 eval_jaxpr.7
  52.7 2.2 eval_jaxpr.8.part_ref
  54.9 1.8 collective-permute-done.2.zl
  56.7 1.2 collective-permute-done.1.yl
  58.4 12.0 %all_to_all.58 = f32[32,4,128]{2,1,0:T(4,128)S(1)} all-to-all(f32[32,4,128]{2,1,0:T(4,128)S(1)} %bitcast.36), channel_id=1, replica_groups=mesh['bx'=4,'by'=8,'bz'=8] {'bx','by'}, dimensions={0} | all-to-all | bytes 131072 | tf_op jit(solution)/shard_map/while/body/eval_jaxpr/all_to_all | solution.py:422
  70.4 9.7 %all_to_all.59 = f32[8,4,128]{2,1,0:T(4,128)S(1)} all-to-all(f32[8,4,128]{2,1,0:T(4,128)S(1)} %broadcast_in_dim.48), channel_id=1, replica_groups=mesh['bx'=4,'by'=8,'bz'=8] {'bz'}, dimensions={0} | all-to-all | bytes 32768 | tf_op jit(solution)/shard_map/while/body/eval_jaxpr/all_to_all | solution.py:422
  80.8 5.4 %all-to-all-start.2 = ((f32[32,4,128]{2,1,0:T(4,128)}), f32[32,4,128]{2,1,0:T(4,128)S(1)}, u32[]{:S(2)}, u32[]{:S(2)}) async-start(f32[32,4,128]{2,1,0:T(4,128)} %broadcast_in_dim.49), calls=%async_computation.2 | async-start | bytes 131072 | tf_op jit(solution)/shard_map/while/body/eval_jaxpr/all_to_all | solution.py:422
  86.2 7.3 %all-to-all-done.2 = f32[32,4,128]{2,1,0:T(4,128)S(1)} async-done(((f32[32,4,128]{2,1,0:T(4,128)}), f32[32,4,128]{2,1,0:T(4,128)S(1)}, u32[]{:S(2)}, u32[]{:S(2)}) %all-to-all-start.2) | async-done | bytes 65568 | tf_op jit(solution)/shard_map/while/body/eval_jaxpr/all_to_all | solution.py:422
  93.5 8.4 %eval_jaxpr.10 = (f32[256,128]{1,0:T(8,128)}, f32[64,1024]{1,0:T(8,128)S(1)}, f32[64,64]{1,0:T(8,128)S(1)}) custom-call(f32[1,1]{1,0:T(1,128)} %get-tuple-element.454.v1_ref, f32[128,128]{1,0:T(8,128)S(1)} %bitcast.37, f32[64,1024]{1,0:T(8,128)S(1)} %get-tuple-element.442.ka, f32[64,1024]{1,0:T(8,128)S(1)} %get-tuple-element.443.kb, ...), custom_call_target="tpu_custom_call" | custom-call | tf_op jit(solution)/shard_map/while/body/eval_jaxpr/pallas_call | solution.py:406
  101.9 3.9 %all-to-all-start.3 = ((f32[32,8,128]{2,1,0:T(8,128)}), f32[32,8,128]{2,1,0:T(8,128)S(1)}, u32[]{:S(2)}, u32[]{:S(2)}) async-start(f32[32,8,128]{2,1,0:T(8,128)} %bitcast.34), calls=%async_computation.3 | async-start | bytes 262144 | tf_op jit(solution)/shard_map/while/body/eval_jaxpr/all_to_all | solution.py:422
  106.2 7.3 %all-to-all-done.3 = f32[32,8,128]{2,1,0:T(8,128)S(1)} async-done(((f32[32,8,128]{2,1,0:T(8,128)}), f32[32,8,128]{2,1,0:T(8,128)S(1)}, u32[]{:S(2)}, u32[]{:S(2)}) %all-to-all-start.3) | async-done | bytes 131104 | tf_op jit(solution)/shard_map/while/body/eval_jaxpr/all_to_all | solution.py:422
  113.5 9.2 %all_to_all.60 = f32[8,8,128]{2,1,0:T(8,128)S(1)} all-to-all(f32[8,8,128]{2,1,0:T(8,128)S(1)} %broadcast_in_dim.50), channel_id=1, replica_groups=mesh['bx'=4,'by'=8,'bz'=8] {'bz'}, dimensions={0} | all-to-all | bytes 65536 | tf_op jit(solution)/shard_map/while/body/eval_jaxpr/all_to_all | solution.py:422
  123.4 5.1 %all-to-all-start.5 = ((f32[32,8,128]{2,1,0:T(8,128)}), f32[32,8,128]{2,1,0:T(8,128)S(1)}, u32[]{:S(2)}, u32[]{:S(2)}) async-start(f32[32,8,128]{2,1,0:T(8,128)} %broadcast_in_dim.51), calls=%async_computation.5 | async-start | bytes 262144 | tf_op jit(solution)/shard_map/while/body/eval_jaxpr/all_to_all | solution.py:422
  128.6 3.6 %collective-permute-start.4 = (f32[64,256]{1,0:T(8,128)S(1)}, f32[64,256]{1,0:T(8,128)S(1)}, u32[]{:S(2)}, u32[]{:S(2)}) collective-permute-start(f32[64,256]{1,0:T(8,128)S(1)} %get-tuple-element.393.yh), channel_id=1, source_target_pairs={{0,56},{8,0},{16,8},{24,16},{32,24},{40,32},{48,40},{56,48},{1,57}... | collective-permute-start | bytes 196616 | tf_op jit(solution)/shard_map/while/body/eval_jaxpr/ppermute | solution.py:469
  132.4 1.5 eval_jaxpr.11
  133.9 1.4 collective-permute-done.5
  136.2 5.4 %eval_jaxpr.6 = (f32[64,1024]{1,0:T(8,128)S(1)}, f32[64,464]{1,0:T(8,128)S(1)}, f32[32,64]{1,0:T(8,128)S(1)}, f32[32,64]{1,0:T(8,128)S(1)}, f32[64,384]{1,0:T(8,...) custom-call(f32[256,128]{1,0:T(8,128)S(1)} %get-tuple-element.432.su, ...), custom_call_target="tpu_custom_call" | custom-call | tf_op jit(solution)/shard_map/while/body/eval_jaxpr/pallas_call | solution.py:406
  141.7 2.9 %collective-permute-start = (f32[64,1024]{1,0:T(8,128)S(1)}, f32[64,1024]{1,0:T(8,128)S(1)}, u32[]{:S(2)}, u32[]{:S(2)}) collective-permute-start(f32[64,1024]{1,0:T(8,128)S(1)} %get-tuple-element.443.kb), channel_id=1, source_target_pairs={{0,64},{64,128},{128,192},{192,0},{1,65},{65,129},{129,193},{193,1... | collective-permute-start | bytes 786440 | tf_op jit(solution)/shard_map/while/body/eval_jaxpr/ppermute | solution.py:469
  144.6 1.3 eval_jaxpr.7
  146.4 2.2 eval_jaxpr.8.part_ref
  148.6 1.5 collective-permute-done.2.zl
  150.1 1.2 collective-permute-done.1.yl
  151.8 12.0 %all_to_all.58 = f32[32,4,128]{2,1,0:T(4,128)S(1)} all-to-all(f32[32,4,128]{2,1,0:T(4,128)S(1)} %bitcast.36), channel_id=1, replica_groups=mesh['bx'=4,'by'=8,'bz'=8] {'bx','by'}, dimensions={0} | all-to-all | bytes 131072 | tf_op jit(solution)/shard_map/while/body/eval_jaxpr/all_to_all | solution.py:422
  163.8 9.0 %all_to_all.59 = f32[8,4,128]{2,1,0:T(4,128)S(1)} all-to-all(f32[8,4,128]{2,1,0:T(4,128)S(1)} %broadcast_in_dim.48), channel_id=1, replica_groups=mesh['bx'=4,'by'=8,'bz'=8] {'bz'}, dimensions={0} | all-to-all | bytes 32768 | tf_op jit(solution)/shard_map/while/body/eval_jaxpr/all_to_all | solution.py:422
  173.5 5.1 %all-to-all-start.2 = ((f32[32,4,128]{2,1,0:T(4,128)}), f32[32,4,128]{2,1,0:T(4,128)S(1)}, u32[]{:S(2)}, u32[]{:S(2)}) async-start(f32[32,4,128]{2,1,0:T(4,128)} %broadcast_in_dim.49), calls=%async_computation.2 | async-start | bytes 131072 | tf_op jit(solution)/shard_map/while/body/eval_jaxpr/all_to_all | solution.py:422
  178.6 7.3 %all-to-all-done.2 = f32[32,4,128]{2,1,0:T(4,128)S(1)} async-done(((f32[32,4,128]{2,1,0:T(4,128)}), f32[32,4,128]{2,1,0:T(4,128)S(1)}, u32[]{:S(2)}, u32[]{:S(2)}) %all-to-all-start.2) | async-done | bytes 65568 | tf_op jit(solution)/shard_map/while/body/eval_jaxpr/all_to_all | solution.py:422
  185.9 8.4 %eval_jaxpr.10 = (f32[256,128]{1,0:T(8,128)}, f32[64,1024]{1,0:T(8,128)S(1)}, f32[64,64]{1,0:T(8,128)S(1)}) custom-call(f32[1,1]{1,0:T(1,128)} %get-tuple-element.454.v1_ref, f32[128,128]{1,0:T(8,128)S(1)} %bitcast.37, f32[64,1024]{1,0:T(8,128)S(1)} %get-tuple-element.442.ka, f32[64,1024]{1,0:T(8,128)S(1)} %get-tuple-element.443.kb, ...), custom_call_target="tpu_custom_call" | custom-call | tf_op jit(solution)/shard_map/while/body/eval_jaxpr/pallas_call | solution.py:406
  194.3 4.0 %all-to-all-start.3 = ((f32[32,8,128]{2,1,0:T(8,128)}), f32[32,8,128]{2,1,0:T(8,128)S(1)}, u32[]{:S(2)}, u32[]{:S(2)}) async-start(f32[32,8,128]{2,1,0:T(8,128)} %bitcast.34), calls=%async_computation.3 | async-start | bytes 262144 | tf_op jit(solution)/shard_map/while/body/eval_jaxpr/all_to_all | solution.py:422
  198.6 7.3 %all-to-all-done.3 = f32[32,8,128]{2,1,0:T(8,128)S(1)} async-done(((f32[32,8,128]{2,1,0:T(8,128)}), f32[32,8,128]{2,1,0:T(8,128)S(1)}, u32[]{:S(2)}, u32[]{:S(2)}) %all-to-all-start.3) | async-done | bytes 131104 | tf_op jit(solution)/shard_map/while/body/eval_jaxpr/all_to_all | solution.py:422
  205.9 9.2 %all_to_all.60 = f32[8,8,128]{2,1,0:T(8,128)S(1)} all-to-all(f32[8,8,128]{2,1,0:T(8,128)S(1)} %broadcast_in_dim.50), channel_id=1, replica_groups=mesh['bx'=4,'by'=8,'bz'=8] {'bz'}, dimensions={0} | all-to-all | bytes 65536 | tf_op jit(solution)/shard_map/while/body/eval_jaxpr/all_to_all | solution.py:422
  215.8 5.1 %all-to-all-start.5 = ((f32[32,8,128]{2,1,0:T(8,128)}), f32[32,8,128]{2,1,0:T(8,128)S(1)}, u32[]{:S(2)}, u32[]{:S(2)}) async-start(f32[32,8,128]{2,1,0:T(8,128)} %broadcast_in_dim.51), calls=%async_computation.5 | async-start | bytes 262144 | tf_op jit(solution)/shard_map/while/body/eval_jaxpr/all_to_all | solution.py:422
  221.0 3.6 %collective-permute-start.4 = (f32[64,256]{1,0:T(8,128)S(1)}, f32[64,256]{1,0:T(8,128)S(1)}, u32[]{:S(2)}, u32[]{:S(2)}) collective-permute-start(f32[64,256]{1,0:T(8,128)S(1)} %get-tuple-element.393.yh), channel_id=1, source_target_pairs={{0,56},{8,0},{16,8},{24,16},{32,24},{40,32},{48,40},{56,48},{1,57}... | collective-permute-start | bytes 196616 | tf_op jit(solution)/shard_map/while/body/eval_jaxpr/ppermute | solution.py:469
  224.8 1.5 eval_jaxpr.11
  226.3 1.4 collective-permute-done.5
  228.6 4.6 %shard_map.68 = (f32[64,64]{1,0:T(8,128)}, f32[64,1024]{1,0:T(8,128)}) custom-call(f32[256,128]{1,0:T(8,128)S(1)} %get-tuple-element.112.sums_ref, f32[64,64]{1,0:T(8,128)S(1)} %get-tuple-element.113.cxi_ref, f32[64,1024]{1,0:T(8,128)S(1)} %get-tuple-element.114.rows_ref, f32[24,1024]{1,0:T(8,128)S(1)} %get-tuple-element.482, f32[160,16]{1,0:T(8,128)S(1)} %get-tuple-element.472), custom_call_target="tpu_custom_call" | custom-call | tf_op jit(solution)/shard_map/pallas_call | solution.py:406
  (73 shorter events, 11.0 us)
Async XLA Ops:
  0.6 1.1 copy-start.1
  2.1 38.9 %collective-permute-start.7 = (f32[64,256]{1,0:T(8,128)S(1)}, f32[64,256]{1,0:T(8,128)S(1)}, u32[]{:S(2)}, u32[]{:S(2)}) collective-permute-start(f32[64,256]{1,0:T(8,128)S(1)} %bitcast.49), channel_id=1, source_target_pairs={{0,8},{8,16},{16,24},{24,32},{32,40},{40,48},{48,56},{56,0},{1,9},... | collective-permute-start | bytes 196616 | tf_op jit(solution)/shard_map/ppermute | solution.py:469
  6.6 15.3 %all-to-all-start.6 = ((f32[32,8,128]{2,1,0:T(8,128)}), f32[32,8,128]{2,1,0:T(8,128)S(1)}, u32[]{:S(2)}, u32[]{:S(2)}) async-start(f32[32,8,128]{2,1,0:T(8,128)} %bitcast.3), calls=%async_computation.6 | async-start | bytes 262144 | tf_op jit(solution)/shard_map/all_to_all | solution.py:422
  14.4 26.6 %collective-permute-start.9 = (f32[64,1024]{1,0:T(8,128)S(1)}, f32[64,1024]{1,0:T(8,128)S(1)}, u32[]{:S(2)}, u32[]{:S(2)}) collective-permute-start(f32[64,1024]{1,0:T(8,128)S(1)} %bitcast.38), channel_id=1, source_target_pairs={{0,192},{64,0},{128,64},{192,128},{1,193},{65,1},{129,65},{193,129... | collective-permute-start | bytes 786440 | tf_op jit(solution)/shard_map/ppermute | solution.py:469
  14.8 26.3 %collective-permute-start.6 = (f32[64,1024]{1,0:T(8,128)S(1)}, f32[64,1024]{1,0:T(8,128)S(1)}, u32[]{:S(2)}, u32[]{:S(2)}) collective-permute-start(f32[64,1024]{1,0:T(8,128)S(1)} %bitcast.40), channel_id=1, source_target_pairs={{0,64},{64,128},{128,192},{192,0},{1,65},{65,129},{129,193},{193,1... | collective-permute-start | bytes 786440 | tf_op jit(solution)/shard_map/ppermute | solution.py:469
  22.6 18.4 %all-to-all-start.7 = ((f32[32,8,128]{2,1,0:T(8,128)}), f32[32,8,128]{2,1,0:T(8,128)S(1)}, u32[]{:S(2)}, u32[]{:S(2)}) async-start(f32[32,8,128]{2,1,0:T(8,128)} %broadcast_in_dim.12), calls=%async_computation.7 | async-start | bytes 262144 | tf_op jit(solution)/shard_map/all_to_all | solution.py:422
  27.1 9.4 %collective-permute-start.11 = (f32[64,128]{0,1:T(8,128)S(1)}, f32[64,128]{0,1:T(8,128)S(1)}, u32[]{:S(2)}, u32[]{:S(2)}) collective-permute-start(f32[64,128]{0,1:T(8,128)S(1)} %concatenate.7), channel_id=1, source_target_pairs={{0,7},{1,0},{2,1},{3,2},{4,3},{5,4},{6,5},{7,6},{8,15},{9,8},{10,9... | collective-permute-start | bytes 98312 | tf_op jit(solution)/shard_map/ppermute | solution.py:469
  32.8 8.3 %collective-permute-start.10 = (f32[64,256]{1,0:T(8,128)S(1)}, f32[64,256]{1,0:T(8,128)S(1)}, u32[]{:S(2)}, u32[]{:S(2)}) collective-permute-start(f32[64,256]{1,0:T(8,128)S(1)} %bitcast.50), channel_id=1, source_target_pairs={{0,56},{8,0},{16,8},{24,16},{32,24},{40,32},{48,40},{56,48},{1,57}... | collective-permute-start | bytes 196616 | tf_op jit(solution)/shard_map/ppermute | solution.py:469
  36.5 0.8 copy-start.2
  36.6 4.4 %collective-permute-start.8 = (f32[64,128]{0,1:T(8,128)S(1)}, f32[64,128]{0,1:T(8,128)S(1)}, u32[]{:S(2)}, u32[]{:S(2)}) collective-permute-start(f32[64,128]{0,1:T(8,128)S(1)} %concatenate.6), channel_id=1, source_target_pairs={{0,1},{1,2},{2,3},{3,4},{4,5},{5,6},{6,7},{7,0},{8,9},{9,10},{10,1... | collective-permute-start | bytes 98312 | tf_op jit(solution)/shard_map/ppermute | solution.py:469
  37.4 3.7 %copy-start = (f32[160,16]{1,0:T(8,128)S(1)}, f32[160,16]{1,0:T(8,128)}, u32[]{:S(2)}) copy-start(f32[160,16]{1,0:T(8,128)} %constant.53.clone.cons_ref) | copy-start | bytes 30724
  46.7 11.1 %collective-permute-start = (f32[64,1024]{1,0:T(8,128)S(1)}, f32[64,1024]{1,0:T(8,128)S(1)}, u32[]{:S(2)}, u32[]{:S(2)}) collective-permute-start(f32[64,1024]{1,0:T(8,128)S(1)} %get-tuple-element.443.kb), channel_id=1, source_target_pairs={{0,64},{64,128},{128,192},{192,0},{1,65},{65,129},{129,193},{193,1... | collective-permute-start | bytes 786440 | tf_op jit(solution)/shard_map/while/body/eval_jaxpr/ppermute | solution.py:469
  52.5 5.3 %collective-permute-start.1 = (f32[64,256]{1,0:T(8,128)S(1)}, f32[64,256]{1,0:T(8,128)S(1)}, u32[]{:S(2)}, u32[]{:S(2)}) collective-permute-start(f32[64,256]{1,0:T(8,128)S(1)} %get-tuple-element.391), channel_id=1, source_target_pairs={{0,8},{8,16},{16,24},{24,32},{32,40},{40,48},{48,56},{56,0},{1,9},... | collective-permute-start | bytes 196616 | tf_op jit(solution)/shard_map/while/body/eval_jaxpr/ppermute | solution.py:469
  52.6 4.1 %collective-permute-start.2 = (f32[64,128]{1,0:T(8,128)S(1)}, f32[64,128]{1,0:T(8,128)S(1)}, u32[]{:S(2)}, u32[]{:S(2)}) collective-permute-start(f32[64,128]{1,0:T(8,128)S(1)} %get-tuple-element.392), channel_id=1, source_target_pairs={{0,1},{1,2},{2,3},{3,4},{4,5},{5,6},{6,7},{7,0},{8,9},{9,10},{10,1... | collective-permute-start | bytes 98312 | tf_op jit(solution)/shard_map/while/body/eval_jaxpr/ppermute | solution.py:469
  80.8 12.7 %all-to-all-start.2 = ((f32[32,4,128]{2,1,0:T(4,128)}), f32[32,4,128]{2,1,0:T(4,128)S(1)}, u32[]{:S(2)}, u32[]{:S(2)}) async-start(f32[32,4,128]{2,1,0:T(4,128)} %broadcast_in_dim.49), calls=%async_computation.2 | async-start | bytes 131072 | tf_op jit(solution)/shard_map/while/body/eval_jaxpr/all_to_all | solution.py:422
  101.9 11.6 %all-to-all-start.3 = ((f32[32,8,128]{2,1,0:T(8,128)}), f32[32,8,128]{2,1,0:T(8,128)S(1)}, u32[]{:S(2)}, u32[]{:S(2)}) async-start(f32[32,8,128]{2,1,0:T(8,128)} %bitcast.34), calls=%async_computation.3 | async-start | bytes 262144 | tf_op jit(solution)/shard_map/while/body/eval_jaxpr/all_to_all | solution.py:422
  105.8 29.4 %collective-permute-start.3 = (f32[64,1024]{1,0:T(8,128)S(1)}, f32[64,1024]{1,0:T(8,128)S(1)}, u32[]{:S(2)}, u32[]{:S(2)}) collective-permute-start(f32[64,1024]{1,0:T(8,128)S(1)} %get-tuple-element.442.ka), channel_id=1, source_target_pairs={{0,192},{64,0},{128,64},{192,128},{1,193},{65,1},{129,65},{193,129... | collective-permute-start | bytes 786440 | tf_op jit(solution)/shard_map/while/body/eval_jaxpr/ppermute | solution.py:469
  123.4 12.8 %all-to-all-start.5 = ((f32[32,8,128]{2,1,0:T(8,128)}), f32[32,8,128]{2,1,0:T(8,128)S(1)}, u32[]{:S(2)}, u32[]{:S(2)}) async-start(f32[32,8,128]{2,1,0:T(8,128)} %broadcast_in_dim.51), calls=%async_computation.5 | async-start | bytes 262144 | tf_op jit(solution)/shard_map/while/body/eval_jaxpr/all_to_all | solution.py:422
  128.6 6.6 %collective-permute-start.4 = (f32[64,256]{1,0:T(8,128)S(1)}, f32[64,256]{1,0:T(8,128)S(1)}, u32[]{:S(2)}, u32[]{:S(2)}) collective-permute-start(f32[64,256]{1,0:T(8,128)S(1)} %get-tuple-element.393.yh), channel_id=1, source_target_pairs={{0,56},{8,0},{16,8},{24,16},{32,24},{40,32},{48,40},{56,48},{1,57}... | collective-permute-start | bytes 196616 | tf_op jit(solution)/shard_map/while/body/eval_jaxpr/ppermute | solution.py:469
  132.2 3.1 %collective-permute-start.5 = (f32[64,128]{1,0:T(8,128)S(1)}, f32[64,128]{1,0:T(8,128)S(1)}, u32[]{:S(2)}, u32[]{:S(2)}) collective-permute-start(f32[64,128]{1,0:T(8,128)S(1)} %get-tuple-element.394.zh), channel_id=1, source_target_pairs={{0,7},{1,0},{2,1},{3,2},{4,3},{5,4},{6,5},{7,6},{8,15},{9,8},{10,9... | collective-permute-start | bytes 98312 | tf_op jit(solution)/shard_map/while/body/eval_jaxpr/ppermute | solution.py:469
  141.7 9.6 %collective-permute-start = (f32[64,1024]{1,0:T(8,128)S(1)}, f32[64,1024]{1,0:T(8,128)S(1)}, u32[]{:S(2)}, u32[]{:S(2)}) collective-permute-start(f32[64,1024]{1,0:T(8,128)S(1)} %get-tuple-element.443.kb), channel_id=1, source_target_pairs={{0,64},{64,128},{128,192},{192,0},{1,65},{65,129},{129,193},{193,1... | collective-permute-start | bytes 786440 | tf_op jit(solution)/shard_map/while/body/eval_jaxpr/ppermute | solution.py:469
  145.9 5.3 %collective-permute-start.1 = (f32[64,256]{1,0:T(8,128)S(1)}, f32[64,256]{1,0:T(8,128)S(1)}, u32[]{:S(2)}, u32[]{:S(2)}) collective-permute-start(f32[64,256]{1,0:T(8,128)S(1)} %get-tuple-element.391), channel_id=1, source_target_pairs={{0,8},{8,16},{16,24},{24,32},{32,40},{40,48},{48,56},{56,0},{1,9},... | collective-permute-start | bytes 196616 | tf_op jit(solution)/shard_map/while/body/eval_jaxpr/ppermute | solution.py:469
  146.0 4.1 %collective-permute-start.2 = (f32[64,128]{1,0:T(8,128)S(1)}, f32[64,128]{1,0:T(8,128)S(1)}, u32[]{:S(2)}, u32[]{:S(2)}) collective-permute-start(f32[64,128]{1,0:T(8,128)S(1)} %get-tuple-element.392), channel_id=1, source_target_pairs={{0,1},{1,2},{2,3},{3,4},{4,5},{5,6},{6,7},{7,0},{8,9},{9,10},{10,1... | collective-permute-start | bytes 98312 | tf_op jit(solution)/shard_map/while/body/eval_jaxpr/ppermute | solution.py:469
  173.5 12.4 %all-to-all-start.2 = ((f32[32,4,128]{2,1,0:T(4,128)}), f32[32,4,128]{2,1,0:T(4,128)S(1)}, u32[]{:S(2)}, u32[]{:S(2)}) async-start(f32[32,4,128]{2,1,0:T(4,128)} %broadcast_in_dim.49), calls=%async_computation.2 | async-start | bytes 131072 | tf_op jit(solution)/shard_map/while/body/eval_jaxpr/all_to_all | solution.py:422
  194.3 11.6 %all-to-all-start.3 = ((f32[32,8,128]{2,1,0:T(8,128)}), f32[32,8,128]{2,1,0:T(8,128)S(1)}, u32[]{:S(2)}, u32[]{:S(2)}) async-start(f32[32,8,128]{2,1,0:T(8,128)} %bitcast.34), calls=%async_computation.3 | async-start | bytes 262144 | tf_op jit(solution)/shard_map/while/body/eval_jaxpr/all_to_all | solution.py:422
  198.2 29.4 %collective-permute-start.3 = (f32[64,1024]{1,0:T(8,128)S(1)}, f32[64,1024]{1,0:T(8,128)S(1)}, u32[]{:S(2)}, u32[]{:S(2)}) collective-permute-start(f32[64,1024]{1,0:T(8,128)S(1)} %get-tuple-element.442.ka), channel_id=1, source_target_pairs={{0,192},{64,0},{128,64},{192,128},{1,193},{65,1},{129,65},{193,129... | collective-permute-start | bytes 786440 | tf_op jit(solution)/shard_map/while/body/eval_jaxpr/ppermute | solution.py:469
  215.8 12.8 %all-to-all-start.5 = ((f32[32,8,128]{2,1,0:T(8,128)}), f32[32,8,128]{2,1,0:T(8,128)S(1)}, u32[]{:S(2)}, u32[]{:S(2)}) async-start(f32[32,8,128]{2,1,0:T(8,128)} %broadcast_in_dim.51), calls=%async_computation.5 | async-start | bytes 262144 | tf_op jit(solution)/shard_map/while/body/eval_jaxpr/all_to_all | solution.py:422
  221.0 6.6 %collective-permute-start.4 = (f32[64,256]{1,0:T(8,128)S(1)}, f32[64,256]{1,0:T(8,128)S(1)}, u32[]{:S(2)}, u32[]{:S(2)}) collective-permute-start(f32[64,256]{1,0:T(8,128)S(1)} %get-tuple-element.393.yh), channel_id=1, source_target_pairs={{0,56},{8,0},{16,8},{24,16},{32,24},{40,32},{48,40},{56,48},{1,57}... | collective-permute-start | bytes 196616 | tf_op jit(solution)/shard_map/while/body/eval_jaxpr/ppermute | solution.py:469
  224.6 3.1 %collective-permute-start.5 = (f32[64,128]{1,0:T(8,128)S(1)}, f32[64,128]{1,0:T(8,128)S(1)}, u32[]{:S(2)}, u32[]{:S(2)}) collective-permute-start(f32[64,128]{1,0:T(8,128)S(1)} %get-tuple-element.394.zh), channel_id=1, source_target_pairs={{0,7},{1,0},{2,1},{3,2},{4,3},{5,4},{6,5},{7,6},{8,15},{9,8},{10,9... | collective-permute-start | bytes 98312 | tf_op jit(solution)/shard_map/while/body/eval_jaxpr/ppermute | solution.py:469

commit v2 on v1

--- a/solution.py
+++ b/solution.py
@@ -398,7 +398,7 @@
     out_ref[...] = mm(civ, rows_ref[...] + mm(gain, tab_ref[0:16, :]))
 
 
-def call(kernel, outs, scratch, *args):
+def call(kernel, outs, scratch, *args, alias=None):
     shapes = [jax.ShapeDtypeStruct(s, F32) for s in outs]
     specs = [pl.BlockSpec(memory_space=pltpu.VMEM) for _ in args]
     if args[0].shape == (1, 1):
@@ -409,6 +409,7 @@
         in_specs=specs,
         out_specs=[pl.BlockSpec(memory_space=pltpu.VMEM) for _ in outs],
         scratch_shapes=[pltpu.VMEM(s, F32) for s in scratch],
+        input_output_aliases=alias or {},
         compiler_params=pltpu.CompilerParams(vmem_limit_bytes=40 * 1024 * 1024),
     )(*args)
 
@@ -505,9 +506,12 @@
             [(256, 128), (RANK, vel_rows), (RANK, RANK)],
             [(408, vel_rows), (320, vel_rows)],
             v1, sums, ka, kb, rows, gain, tab, cons, gw, mode_rows, moments, civ, ginv,
+            alias={4: 1},
         )
         (space,) = call(space_kernel, [shape], [], base, ka, kb)
-        sums = plane_gather(line_sum(plane_sum(payload)))
+        part = plane_sum(payload)
+        part = line_sum(part)
+        sums = plane_gather(part)
         return ka, kb, low, high, sums, rows, base, space
 
     carry = (fa, fb, low, high, sums, velocity_factor, core_matrix.T, jnp.zeros(shape, F32))

time: 234 us -> 232 us (level)
  blocking collectives: 61.2 us -> 85.5 us
  waiting for transfers between devices: 47.1 us -> 32.5 us
  starting transfers between devices: 71.3 us -> 60.9 us
    all_to_all x6 -> x8, blocking collectives: 61.2 us -> 85.5 us  [swap(): return lax.all_to_all(chunks, axis, 0, 0, tiled=True)]
    all_to_all x8 -> x6, waiting for transfers between devices: 35.1 us -> 20.5 us  [swap(): return lax.all_to_all(chunks, axis, 0, 0, tiled=True)]
    all_to_all x8 -> x6, starting transfers between devices: 40.4 us -> 30 us  [swap(): return lax.all_to_all(chunks, axis, 0, 0, tiled=True)]
  transfers between devices with their start and end apart: 26 -> 24, of which waited for: 14 -> 12; matrix products, arithmetic and copies ran while one was open for 1% -> 1% of each run, Pallas kernels for 5% -> 5%
where the time goes in v2:
time: 232 us; the launch traced here: 231 us
  blocking collectives  85.5 us (37%)
  starting transfers between devices  60.9 us (26%)
  Pallas kernels  45.5 us (20%)
  waiting for transfers between devices  32.5 us (14%)
  local copies, waits for them, and re-layouts  5.41 us (2%)
    all_to_all x8, blocking collectives, swap(): return lax.all_to_all(chunks, axis, 0, 0, tiled=True)  85.5 us
    pallas_call x14, Pallas kernels, call(): pl.pallas_call(kernel, out_shape=shapes, in_specs=specs, out_specs=[pl.Bl...  45.5 us
    ppermute x18, starting transfers between devices, halo(): out.append(lax.ppermute(field, axis, route(axis, step)))  30.9 us
    all_to_all x6, starting transfers between devices, swap(): return lax.all_to_all(chunks, axis, 0, 0, tiled=True)  30 us
    all_to_all x6, waiting for transfers between devices, swap(): return lax.all_to_all(chunks, axis, 0, 0, tiled=True)  20.5 us
    ppermute x18, waiting for transfers between devices, halo(): out.append(lax.ppermute(field, axis, route(axis, step)))  11.9 us
  transfers between devices with their start and end apart: 24, of which 12 were waited for; matrix products, arithmetic and copies ran while one was open for 1% of the time, Pallas kernels for 5%

profile of v2, /device:TPU:1, one launch (start us, length us, event | category | flops | bytes accessed | tf_op | source)
XLA Modules:
  0.0 231.1 jit_solution(2871140713891823050)
XLA Ops:
  0.6 1.0 copy.82.rows_ref
  2.1 2.1 collective-permute-start.7
  4.3 2.3 %shard_map.67 = (f32[256,128]{1,0:T(8,128)}, f32[24,1024]{1,0:T(8,128)S(1)}) custom-call(f32[1,1]{1,0:T(1,128)} %bitcast.2.v1_ref, f32[64,1024]{1,0:T(8,128)S(1)} %copy.82.rows_ref), custom_call_target="tpu_custom_call" | custom-call | tf_op jit(solution)/shard_map/pallas_call | solution.py:406
  6.6 7.8 %all-to-all-start.6 = ((f32[32,8,128]{2,1,0:T(8,128)}), f32[32,8,128]{2,1,0:T(8,128)S(1)}, u32[]{:S(2)}, u32[]{:S(2)}) async-start(f32[32,8,128]{2,1,0:T(8,128)} %bitcast.3), calls=%async_computation.6 | async-start | bytes 262144 | tf_op jit(solution)/shard_map/all_to_all | solution.py:423
  14.8 3.1 %collective-permute-start.6 = (f32[64,1024]{1,0:T(8,128)S(1)}, f32[64,1024]{1,0:T(8,128)S(1)}, u32[]{:S(2)}, u32[]{:S(2)}) collective-permute-start(f32[64,1024]{1,0:T(8,128)S(1)} %bitcast.40), channel_id=1, source_target_pairs={{0,64},{64,128},{128,192},{192,0},{1,65},{65,129},{129,193},{193,1... | collective-permute-start | bytes 786440 | tf_op jit(solution)/shard_map/ppermute | solution.py:470
  17.9 4.0 %all-to-all-done.6 = f32[32,8,128]{2,1,0:T(8,128)S(1)} async-done(((f32[32,8,128]{2,1,0:T(8,128)}), f32[32,8,128]{2,1,0:T(8,128)S(1)}, u32[]{:S(2)}, u32[]{:S(2)}) %all-to-all-start.6) | async-done | bytes 131104 | tf_op jit(solution)/shard_map/all_to_all | solution.py:423
  22.6 4.0 %all-to-all-start.7 = ((f32[32,8,128]{2,1,0:T(8,128)}), f32[32,8,128]{2,1,0:T(8,128)S(1)}, u32[]{:S(2)}, u32[]{:S(2)}) async-start(f32[32,8,128]{2,1,0:T(8,128)} %broadcast_in_dim.12), calls=%async_computation.7 | async-start | bytes 262144 | tf_op jit(solution)/shard_map/all_to_all | solution.py:423
  27.1 5.6 %collective-permute-start.11 = (f32[64,128]{0,1:T(8,128)S(1)}, f32[64,128]{0,1:T(8,128)S(1)}, u32[]{:S(2)}, u32[]{:S(2)}) collective-permute-start(f32[64,128]{0,1:T(8,128)S(1)} %concatenate.7), channel_id=1, source_target_pairs={{0,7},{1,0},{2,1},{3,2},{4,3},{5,4},{6,5},{7,6},{8,15},{9,8},{10,9... | collective-permute-start | bytes 98312 | tf_op jit(solution)/shard_map/ppermute | solution.py:470
  32.8 3.5 %collective-permute-start.10 = (f32[64,256]{1,0:T(8,128)S(1)}, f32[64,256]{1,0:T(8,128)S(1)}, u32[]{:S(2)}, u32[]{:S(2)}) collective-permute-start(f32[64,256]{1,0:T(8,128)S(1)} %bitcast.50), channel_id=1, source_target_pairs={{0,56},{8,0},{16,8},{24,16},{32,24},{40,32},{48,40},{56,48},{1,57}... | collective-permute-start | bytes 196616 | tf_op jit(solution)/shard_map/ppermute | solution.py:470
  37.4 3.5 %collective-permute-done.8 = f32[64,128]{0,1:T(8,128)S(1)} collective-permute-done((f32[64,128]{0,1:T(8,128)S(1)}, f32[64,128]{0,1:T(8,128)S(1)}, u32[]{:S(2)}, u32[]{:S(2)}) %collective-permute-start.8) | collective-permute-done | bytes 32800 | tf_op jit(solution)/shard_map/ppermute | solution.py:470
  41.1 185.4 %while.33 = (s32[]{:T(128)}, f32[64,1024]{1,0:T(8,128)S(1)}, f32[64,1024]{1,0:T(8,128)S(1)}, f32[64,1024]{1,0:T(8,128)S(1)}, f32[64,256]{1,0:T(8,128)S(1)}, /*in...) while((s32[]{:T(128)}, f32[64,1024]{1,0:T(8,128)S(1)}, ...), condition=%wide.region_6.7_spmd.clone, body=%wide.region_1.6_spmd.sunk.clone.sunk | while | flops 58370 | bytes 6119909 | solution.py:518
  41.3 5.4 %eval_jaxpr.6 = (f32[64,1024]{1,0:T(8,128)S(1)}, f32[64,464]{1,0:T(8,128)S(1)}, f32[32,64]{1,0:T(8,128)S(1)}, f32[32,64]{1,0:T(8,128)S(1)}, f32[64,384]{1,0:T(8,...) custom-call(f32[256,128]{1,0:T(8,128)S(1)} %get-tuple-element.432.su, ...), custom_call_target="tpu_custom_call" | custom-call | tf_op jit(solution)/shard_map/while/body/eval_jaxpr/pallas_call | solution.py:406
  46.7 4.5 %collective-permute-start = (f32[64,1024]{1,0:T(8,128)S(1)}, f32[64,1024]{1,0:T(8,128)S(1)}, u32[]{:S(2)}, u32[]{:S(2)}) collective-permute-start(f32[64,1024]{1,0:T(8,128)S(1)} %get-tuple-element.443.kb), channel_id=1, source_target_pairs={{0,64},{64,128},{128,192},{192,0},{1,65},{65,129},{129,193},{193,1... | collective-permute-start | bytes 786440 | tf_op jit(solution)/shard_map/while/body/eval_jaxpr/ppermute | solution.py:470
  51.2 1.3 eval_jaxpr.7
  52.7 2.2 eval_jaxpr.8.part_ref
  54.9 1.8 collective-permute-done.2.zl
  56.7 1.2 collective-permute-done.1.yl
  58.4 12.0 %all_to_all.58 = f32[32,4,128]{2,1,0:T(4,128)S(1)} all-to-all(f32[32,4,128]{2,1,0:T(4,128)S(1)} %bitcast.36), channel_id=1, replica_groups=mesh['bx'=4,'by'=8,'bz'=8] {'bx','by'}, dimensions={0} | all-to-all | bytes 131072 | tf_op jit(solution)/shard_map/while/body/eval_jaxpr/all_to_all | solution.py:423
  70.4 9.7 %all_to_all.59 = f32[8,4,128]{2,1,0:T(4,128)S(1)} all-to-all(f32[8,4,128]{2,1,0:T(4,128)S(1)} %broadcast_in_dim.48), channel_id=1, replica_groups=mesh['bx'=4,'by'=8,'bz'=8] {'bz'}, dimensions={0} | all-to-all | bytes 32768 | tf_op jit(solution)/shard_map/while/body/eval_jaxpr/all_to_all | solution.py:423
  80.2 12.3 %all_to_all.60 = f32[32,4,128]{2,1,0:T(4,128)S(1)} all-to-all(f32[32,4,128]{2,1,0:T(4,128)S(1)} %broadcast_in_dim.49), channel_id=1, replica_groups=mesh['bx'=4,'by'=8,'bz'=8] {'bx','by'}, dimensions={0} | all-to-all | bytes 131072 | tf_op jit(solution)/shard_map/while/body/eval_jaxpr/all_to_all | solution.py:423
  92.5 8.4 %eval_jaxpr.10 = (f32[256,128]{1,0:T(8,128)}, f32[64,1024]{1,0:T(8,128)S(1)}, f32[64,64]{1,0:T(8,128)S(1)}) custom-call(f32[1,1]{1,0:T(1,128)} %get-tuple-element.454.v1_ref, f32[128,128]{1,0:T(8,128)S(1)} %bitcast.37, f32[64,1024]{1,0:T(8,128)S(1)} %get-tuple-element.442.ka, f32[64,1024]{1,0:T(8,128)S(1)} %get-tuple-element.443.kb, ...), custom_call_target="tpu_custom_call", output_to_operand_aliasing={{1}: (4, {})} | custom-call | tf_op jit(solution)/shard_map/while/body/eval_jaxpr/pallas_call | solution.py:406
  100.8 4.0 %all-to-all-start.3 = ((f32[32,8,128]{2,1,0:T(8,128)}), f32[32,8,128]{2,1,0:T(8,128)S(1)}, u32[]{:S(2)}, u32[]{:S(2)}) async-start(f32[32,8,128]{2,1,0:T(8,128)} %bitcast.34), calls=%async_computation.3 | async-start | bytes 262144 | tf_op jit(solution)/shard_map/while/body/eval_jaxpr/all_to_all | solution.py:423
  105.2 7.3 %all-to-all-done.3 = f32[32,8,128]{2,1,0:T(8,128)S(1)} async-done(((f32[32,8,128]{2,1,0:T(8,128)}), f32[32,8,128]{2,1,0:T(8,128)S(1)}, u32[]{:S(2)}, u32[]{:S(2)}) %all-to-all-start.3) | async-done | bytes 131104 | tf_op jit(solution)/shard_map/while/body/eval_jaxpr/all_to_all | solution.py:423
  112.5 9.2 %all_to_all.61 = f32[8,8,128]{2,1,0:T(8,128)S(1)} all-to-all(f32[8,8,128]{2,1,0:T(8,128)S(1)} %broadcast_in_dim.50), channel_id=1, replica_groups=mesh['bx'=4,'by'=8,'bz'=8] {'bz'}, dimensions={0} | all-to-all | bytes 65536 | tf_op jit(solution)/shard_map/while/body/eval_jaxpr/all_to_all | solution.py:423
  122.4 5.1 %all-to-all-start.5 = ((f32[32,8,128]{2,1,0:T(8,128)}), f32[32,8,128]{2,1,0:T(8,128)S(1)}, u32[]{:S(2)}, u32[]{:S(2)}) async-start(f32[32,8,128]{2,1,0:T(8,128)} %broadcast_in_dim.51), calls=%async_computation.5 | async-start | bytes 262144 | tf_op jit(solution)/shard_map/while/body/eval_jaxpr/all_to_all | solution.py:423
  127.5 3.6 %collective-permute-start.4 = (f32[64,256]{1,0:T(8,128)S(1)}, f32[64,256]{1,0:T(8,128)S(1)}, u32[]{:S(2)}, u32[]{:S(2)}) collective-permute-start(f32[64,256]{1,0:T(8,128)S(1)} %get-tuple-element.393.yh), channel_id=1, source_target_pairs={{0,56},{8,0},{16,8},{24,16},{32,24},{40,32},{48,40},{56,48},{1,57}... | collective-permute-start | bytes 196616 | tf_op jit(solution)/shard_map/while/body/eval_jaxpr/ppermute | solution.py:470
  131.3 1.5 eval_jaxpr.11
  132.8 1.4 collective-permute-done.5
  134.2 1.0 all-to-all-done.5
  135.2 5.4 %eval_jaxpr.6 = (f32[64,1024]{1,0:T(8,128)S(1)}, f32[64,464]{1,0:T(8,128)S(1)}, f32[32,64]{1,0:T(8,128)S(1)}, f32[32,64]{1,0:T(8,128)S(1)}, f32[64,384]{1,0:T(8,...) custom-call(f32[256,128]{1,0:T(8,128)S(1)} %get-tuple-element.432.su, ...), custom_call_target="tpu_custom_call" | custom-call | tf_op jit(solution)/shard_map/while/body/eval_jaxpr/pallas_call | solution.py:406
  140.6 2.9 %collective-permute-start = (f32[64,1024]{1,0:T(8,128)S(1)}, f32[64,1024]{1,0:T(8,128)S(1)}, u32[]{:S(2)}, u32[]{:S(2)}) collective-permute-start(f32[64,1024]{1,0:T(8,128)S(1)} %get-tuple-element.443.kb), channel_id=1, source_target_pairs={{0,64},{64,128},{128,192},{192,0},{1,65},{65,129},{129,193},{193,1... | collective-permute-start | bytes 786440 | tf_op jit(solution)/shard_map/while/body/eval_jaxpr/ppermute | solution.py:470
  143.6 1.3 eval_jaxpr.7
  145.3 2.2 eval_jaxpr.8.part_ref
  147.5 1.5 collective-permute-done.2.zl
  149.0 1.2 collective-permute-done.1.yl
  150.7 12.0 %all_to_all.58 = f32[32,4,128]{2,1,0:T(4,128)S(1)} all-to-all(f32[32,4,128]{2,1,0:T(4,128)S(1)} %bitcast.36), channel_id=1, replica_groups=mesh['bx'=4,'by'=8,'bz'=8] {'bx','by'}, dimensions={0} | all-to-all | bytes 131072 | tf_op jit(solution)/shard_map/while/body/eval_jaxpr/all_to_all | solution.py:423
  162.8 9.0 %all_to_all.59 = f32[8,4,128]{2,1,0:T(4,128)S(1)} all-to-all(f32[8,4,128]{2,1,0:T(4,128)S(1)} %broadcast_in_dim.48), channel_id=1, replica_groups=mesh['bx'=4,'by'=8,'bz'=8] {'bz'}, dimensions={0} | all-to-all | bytes 32768 | tf_op jit(solution)/shard_map/while/body/eval_jaxpr/all_to_all | solution.py:423
  171.8 12.0 %all_to_all.60 = f32[32,4,128]{2,1,0:T(4,128)S(1)} all-to-all(f32[32,4,128]{2,1,0:T(4,128)S(1)} %broadcast_in_dim.49), channel_id=1, replica_groups=mesh['bx'=4,'by'=8,'bz'=8] {'bx','by'}, dimensions={0} | all-to-all | bytes 131072 | tf_op jit(solution)/shard_map/while/body/eval_jaxpr/all_to_all | solution.py:423
  183.8 8.4 %eval_jaxpr.10 = (f32[256,128]{1,0:T(8,128)}, f32[64,1024]{1,0:T(8,128)S(1)}, f32[64,64]{1,0:T(8,128)S(1)}) custom-call(f32[1,1]{1,0:T(1,128)} %get-tuple-element.454.v1_ref, f32[128,128]{1,0:T(8,128)S(1)} %bitcast.37, f32[64,1024]{1,0:T(8,128)S(1)} %get-tuple-element.442.ka, f32[64,1024]{1,0:T(8,128)S(1)} %get-tuple-element.443.kb, ...), custom_call_target="tpu_custom_call", output_to_operand_aliasing={{1}: (4, {})} | custom-call | tf_op jit(solution)/shard_map/while/body/eval_jaxpr/pallas_call | solution.py:406
  192.2 3.9 %all-to-all-start.3 = ((f32[32,8,128]{2,1,0:T(8,128)}), f32[32,8,128]{2,1,0:T(8,128)S(1)}, u32[]{:S(2)}, u32[]{:S(2)}) async-start(f32[32,8,128]{2,1,0:T(8,128)} %bitcast.34), calls=%async_computation.3 | async-start | bytes 262144 | tf_op jit(solution)/shard_map/while/body/eval_jaxpr/all_to_all | solution.py:423
  196.5 7.3 %all-to-all-done.3 = f32[32,8,128]{2,1,0:T(8,128)S(1)} async-done(((f32[32,8,128]{2,1,0:T(8,128)}), f32[32,8,128]{2,1,0:T(8,128)S(1)}, u32[]{:S(2)}, u32[]{:S(2)}) %all-to-all-start.3) | async-done | bytes 131104 | tf_op jit(solution)/shard_map/while/body/eval_jaxpr/all_to_all | solution.py:423
  203.8 9.2 %all_to_all.61 = f32[8,8,128]{2,1,0:T(8,128)S(1)} all-to-all(f32[8,8,128]{2,1,0:T(8,128)S(1)} %broadcast_in_dim.50), channel_id=1, replica_groups=mesh['bx'=4,'by'=8,'bz'=8] {'bz'}, dimensions={0} | all-to-all | bytes 65536 | tf_op jit(solution)/shard_map/while/body/eval_jaxpr/all_to_all | solution.py:423
  213.7 5.1 %all-to-all-start.5 = ((f32[32,8,128]{2,1,0:T(8,128)}), f32[32,8,128]{2,1,0:T(8,128)S(1)}, u32[]{:S(2)}, u32[]{:S(2)}) async-start(f32[32,8,128]{2,1,0:T(8,128)} %broadcast_in_dim.51), calls=%async_computation.5 | async-start | bytes 262144 | tf_op jit(solution)/shard_map/while/body/eval_jaxpr/all_to_all | solution.py:423
  218.9 3.6 %collective-permute-start.4 = (f32[64,256]{1,0:T(8,128)S(1)}, f32[64,256]{1,0:T(8,128)S(1)}, u32[]{:S(2)}, u32[]{:S(2)}) collective-permute-start(f32[64,256]{1,0:T(8,128)S(1)} %get-tuple-element.393.yh), channel_id=1, source_target_pairs={{0,56},{8,0},{16,8},{24,16},{32,24},{40,32},{48,40},{56,48},{1,57}... | collective-permute-start | bytes 196616 | tf_op jit(solution)/shard_map/while/body/eval_jaxpr/ppermute | solution.py:470
  222.6 1.5 eval_jaxpr.11
  224.2 1.4 collective-permute-done.5
  225.5 1.0 all-to-all-done.5
  226.5 4.6 %shard_map.68 = (f32[64,64]{1,0:T(8,128)}, f32[64,1024]{1,0:T(8,128)}) custom-call(f32[256,128]{1,0:T(8,128)S(1)} %get-tuple-element.112.sums_ref, f32[64,64]{1,0:T(8,128)S(1)} %get-tuple-element.113.cxi_ref, f32[64,1024]{1,0:T(8,128)S(1)} %get-tuple-element.114.rows_ref, f32[24,1024]{1,0:T(8,128)S(1)} %get-tuple-element.481, f32[160,16]{1,0:T(8,128)S(1)} %get-tuple-element.471), custom_call_target="tpu_custom_call" | custom-call | tf_op jit(solution)/shard_map/pallas_call | solution.py:406
  (69 shorter events, 7.7 us)
Async XLA Ops:
  0.6 1.1 copy-start.1
  2.1 38.9 %collective-permute-start.7 = (f32[64,256]{1,0:T(8,128)S(1)}, f32[64,256]{1,0:T(8,128)S(1)}, u32[]{:S(2)}, u32[]{:S(2)}) collective-permute-start(f32[64,256]{1,0:T(8,128)S(1)} %bitcast.49), channel_id=1, source_target_pairs={{0,8},{8,16},{16,24},{24,32},{32,40},{40,48},{48,56},{56,0},{1,9},... | collective-permute-start | bytes 196616 | tf_op jit(solution)/shard_map/ppermute | solution.py:470
  6.6 15.3 %all-to-all-start.6 = ((f32[32,8,128]{2,1,0:T(8,128)}), f32[32,8,128]{2,1,0:T(8,128)S(1)}, u32[]{:S(2)}, u32[]{:S(2)}) async-start(f32[32,8,128]{2,1,0:T(8,128)} %bitcast.3), calls=%async_computation.6 | async-start | bytes 262144 | tf_op jit(solution)/shard_map/all_to_all | solution.py:423
  14.4 26.6 %collective-permute-start.9 = (f32[64,1024]{1,0:T(8,128)S(1)}, f32[64,1024]{1,0:T(8,128)S(1)}, u32[]{:S(2)}, u32[]{:S(2)}) collective-permute-start(f32[64,1024]{1,0:T(8,128)S(1)} %bitcast.38), channel_id=1, source_target_pairs={{0,192},{64,0},{128,64},{192,128},{1,193},{65,1},{129,65},{193,129... | collective-permute-start | bytes 786440 | tf_op jit(solution)/shard_map/ppermute | solution.py:470
  14.8 26.3 %collective-permute-start.6 = (f32[64,1024]{1,0:T(8,128)S(1)}, f32[64,1024]{1,0:T(8,128)S(1)}, u32[]{:S(2)}, u32[]{:S(2)}) collective-permute-start(f32[64,1024]{1,0:T(8,128)S(1)} %bitcast.40), channel_id=1, source_target_pairs={{0,64},{64,128},{128,192},{192,0},{1,65},{65,129},{129,193},{193,1... | collective-permute-start | bytes 786440 | tf_op jit(solution)/shard_map/ppermute | solution.py:470
  22.6 18.4 %all-to-all-start.7 = ((f32[32,8,128]{2,1,0:T(8,128)}), f32[32,8,128]{2,1,0:T(8,128)S(1)}, u32[]{:S(2)}, u32[]{:S(2)}) async-start(f32[32,8,128]{2,1,0:T(8,128)} %broadcast_in_dim.12), calls=%async_computation.7 | async-start | bytes 262144 | tf_op jit(solution)/shard_map/all_to_all | solution.py:423
  27.1 9.4 %collective-permute-start.11 = (f32[64,128]{0,1:T(8,128)S(1)}, f32[64,128]{0,1:T(8,128)S(1)}, u32[]{:S(2)}, u32[]{:S(2)}) collective-permute-start(f32[64,128]{0,1:T(8,128)S(1)} %concatenate.7), channel_id=1, source_target_pairs={{0,7},{1,0},{2,1},{3,2},{4,3},{5,4},{6,5},{7,6},{8,15},{9,8},{10,9... | collective-permute-start | bytes 98312 | tf_op jit(solution)/shard_map/ppermute | solution.py:470
  32.8 8.3 %collective-permute-start.10 = (f32[64,256]{1,0:T(8,128)S(1)}, f32[64,256]{1,0:T(8,128)S(1)}, u32[]{:S(2)}, u32[]{:S(2)}) collective-permute-start(f32[64,256]{1,0:T(8,128)S(1)} %bitcast.50), channel_id=1, source_target_pairs={{0,56},{8,0},{16,8},{24,16},{32,24},{40,32},{48,40},{56,48},{1,57}... | collective-permute-start | bytes 196616 | tf_op jit(solution)/shard_map/ppermute | solution.py:470
  36.5 0.8 copy-start.2
  36.6 4.4 %collective-permute-start.8 = (f32[64,128]{0,1:T(8,128)S(1)}, f32[64,128]{0,1:T(8,128)S(1)}, u32[]{:S(2)}, u32[]{:S(2)}) collective-permute-start(f32[64,128]{0,1:T(8,128)S(1)} %concatenate.6), channel_id=1, source_target_pairs={{0,1},{1,2},{2,3},{3,4},{4,5},{5,6},{6,7},{7,0},{8,9},{9,10},{10,1... | collective-permute-start | bytes 98312 | tf_op jit(solution)/shard_map/ppermute | solution.py:470
  37.4 3.7 %copy-start = (f32[160,16]{1,0:T(8,128)S(1)}, f32[160,16]{1,0:T(8,128)}, u32[]{:S(2)}) copy-start(f32[160,16]{1,0:T(8,128)} %constant.53.clone.cons_ref) | copy-start | bytes 30724
  46.7 11.1 %collective-permute-start = (f32[64,1024]{1,0:T(8,128)S(1)}, f32[64,1024]{1,0:T(8,128)S(1)}, u32[]{:S(2)}, u32[]{:S(2)}) collective-permute-start(f32[64,1024]{1,0:T(8,128)S(1)} %get-tuple-element.443.kb), channel_id=1, source_target_pairs={{0,64},{64,128},{128,192},{192,0},{1,65},{65,129},{129,193},{193,1... | collective-permute-start | bytes 786440 | tf_op jit(solution)/shard_map/while/body/eval_jaxpr/ppermute | solution.py:470
  52.5 5.3 %collective-permute-start.1 = (f32[64,256]{1,0:T(8,128)S(1)}, f32[64,256]{1,0:T(8,128)S(1)}, u32[]{:S(2)}, u32[]{:S(2)}) collective-permute-start(f32[64,256]{1,0:T(8,128)S(1)} %get-tuple-element.391), channel_id=1, source_target_pairs={{0,8},{8,16},{16,24},{24,32},{32,40},{40,48},{48,56},{56,0},{1,9},... | collective-permute-start | bytes 196616 | tf_op jit(solution)/shard_map/while/body/eval_jaxpr/ppermute | solution.py:470
  52.6 4.1 %collective-permute-start.2 = (f32[64,128]{1,0:T(8,128)S(1)}, f32[64,128]{1,0:T(8,128)S(1)}, u32[]{:S(2)}, u32[]{:S(2)}) collective-permute-start(f32[64,128]{1,0:T(8,128)S(1)} %get-tuple-element.392), channel_id=1, source_target_pairs={{0,1},{1,2},{2,3},{3,4},{4,5},{5,6},{6,7},{7,0},{8,9},{9,10},{10,1... | collective-permute-start | bytes 98312 | tf_op jit(solution)/shard_map/while/body/eval_jaxpr/ppermute | solution.py:470
  100.8 11.6 %all-to-all-start.3 = ((f32[32,8,128]{2,1,0:T(8,128)}), f32[32,8,128]{2,1,0:T(8,128)S(1)}, u32[]{:S(2)}, u32[]{:S(2)}) async-start(f32[32,8,128]{2,1,0:T(8,128)} %bitcast.34), calls=%async_computation.3 | async-start | bytes 262144 | tf_op jit(solution)/shard_map/while/body/eval_jaxpr/all_to_all | solution.py:423
  104.8 29.4 %collective-permute-start.3 = (f32[64,1024]{1,0:T(8,128)S(1)}, f32[64,1024]{1,0:T(8,128)S(1)}, u32[]{:S(2)}, u32[]{:S(2)}) collective-permute-start(f32[64,1024]{1,0:T(8,128)S(1)} %get-tuple-element.442.ka), channel_id=1, source_target_pairs={{0,192},{64,0},{128,64},{192,128},{1,193},{65,1},{129,65},{193,129... | collective-permute-start | bytes 786440 | tf_op jit(solution)/shard_map/while/body/eval_jaxpr/ppermute | solution.py:470
  122.4 12.8 %all-to-all-start.5 = ((f32[32,8,128]{2,1,0:T(8,128)}), f32[32,8,128]{2,1,0:T(8,128)S(1)}, u32[]{:S(2)}, u32[]{:S(2)}) async-start(f32[32,8,128]{2,1,0:T(8,128)} %broadcast_in_dim.51), calls=%async_computation.5 | async-start | bytes 262144 | tf_op jit(solution)/shard_map/while/body/eval_jaxpr/all_to_all | solution.py:423
  127.5 6.6 %collective-permute-start.4 = (f32[64,256]{1,0:T(8,128)S(1)}, f32[64,256]{1,0:T(8,128)S(1)}, u32[]{:S(2)}, u32[]{:S(2)}) collective-permute-start(f32[64,256]{1,0:T(8,128)S(1)} %get-tuple-element.393.yh), channel_id=1, source_target_pairs={{0,56},{8,0},{16,8},{24,16},{32,24},{40,32},{48,40},{56,48},{1,57}... | collective-permute-start | bytes 196616 | tf_op jit(solution)/shard_map/while/body/eval_jaxpr/ppermute | solution.py:470
  131.1 3.1 %collective-permute-start.5 = (f32[64,128]{1,0:T(8,128)S(1)}, f32[64,128]{1,0:T(8,128)S(1)}, u32[]{:S(2)}, u32[]{:S(2)}) collective-permute-start(f32[64,128]{1,0:T(8,128)S(1)} %get-tuple-element.394.zh), channel_id=1, source_target_pairs={{0,7},{1,0},{2,1},{3,2},{4,3},{5,4},{6,5},{7,6},{8,15},{9,8},{10,9... | collective-permute-start | bytes 98312 | tf_op jit(solution)/shard_map/while/body/eval_jaxpr/ppermute | solution.py:470
  140.6 9.6 %collective-permute-start = (f32[64,1024]{1,0:T(8,128)S(1)}, f32[64,1024]{1,0:T(8,128)S(1)}, u32[]{:S(2)}, u32[]{:S(2)}) collective-permute-start(f32[64,1024]{1,0:T(8,128)S(1)} %get-tuple-element.443.kb), channel_id=1, source_target_pairs={{0,64},{64,128},{128,192},{192,0},{1,65},{65,129},{129,193},{193,1... | collective-permute-start | bytes 786440 | tf_op jit(solution)/shard_map/while/body/eval_jaxpr/ppermute | solution.py:470
  144.9 5.3 %collective-permute-start.1 = (f32[64,256]{1,0:T(8,128)S(1)}, f32[64,256]{1,0:T(8,128)S(1)}, u32[]{:S(2)}, u32[]{:S(2)}) collective-permute-start(f32[64,256]{1,0:T(8,128)S(1)} %get-tuple-element.391), channel_id=1, source_target_pairs={{0,8},{8,16},{16,24},{24,32},{32,40},{40,48},{48,56},{56,0},{1,9},... | collective-permute-start | bytes 196616 | tf_op jit(solution)/shard_map/while/body/eval_jaxpr/ppermute | solution.py:470
  145.0 4.1 %collective-permute-start.2 = (f32[64,128]{1,0:T(8,128)S(1)}, f32[64,128]{1,0:T(8,128)S(1)}, u32[]{:S(2)}, u32[]{:S(2)}) collective-permute-start(f32[64,128]{1,0:T(8,128)S(1)} %get-tuple-element.392), channel_id=1, source_target_pairs={{0,1},{1,2},{2,3},{3,4},{4,5},{5,6},{6,7},{7,0},{8,9},{9,10},{10,1... | collective-permute-start | bytes 98312 | tf_op jit(solution)/shard_map/while/body/eval_jaxpr/ppermute | solution.py:470
  192.2 11.6 %all-to-all-start.3 = ((f32[32,8,128]{2,1,0:T(8,128)}), f32[32,8,128]{2,1,0:T(8,128)S(1)}, u32[]{:S(2)}, u32[]{:S(2)}) async-start(f32[32,8,128]{2,1,0:T(8,128)} %bitcast.34), calls=%async_computation.3 | async-start | bytes 262144 | tf_op jit(solution)/shard_map/while/body/eval_jaxpr/all_to_all | solution.py:423
  196.1 29.4 %collective-permute-start.3 = (f32[64,1024]{1,0:T(8,128)S(1)}, f32[64,1024]{1,0:T(8,128)S(1)}, u32[]{:S(2)}, u32[]{:S(2)}) collective-permute-start(f32[64,1024]{1,0:T(8,128)S(1)} %get-tuple-element.442.ka), channel_id=1, source_target_pairs={{0,192},{64,0},{128,64},{192,128},{1,193},{65,1},{129,65},{193,129... | collective-permute-start | bytes 786440 | tf_op jit(solution)/shard_map/while/body/eval_jaxpr/ppermute | solution.py:470
  213.7 12.8 %all-to-all-start.5 = ((f32[32,8,128]{2,1,0:T(8,128)}), f32[32,8,128]{2,1,0:T(8,128)S(1)}, u32[]{:S(2)}, u32[]{:S(2)}) async-start(f32[32,8,128]{2,1,0:T(8,128)} %broadcast_in_dim.51), calls=%async_computation.5 | async-start | bytes 262144 | tf_op jit(solution)/shard_map/while/body/eval_jaxpr/all_to_all | solution.py:423
  218.9 6.6 %collective-permute-start.4 = (f32[64,256]{1,0:T(8,128)S(1)}, f32[64,256]{1,0:T(8,128)S(1)}, u32[]{:S(2)}, u32[]{:S(2)}) collective-permute-start(f32[64,256]{1,0:T(8,128)S(1)} %get-tuple-element.393.yh), channel_id=1, source_target_pairs={{0,56},{8,0},{16,8},{24,16},{32,24},{40,32},{48,40},{56,48},{1,57}... | collective-permute-start | bytes 196616 | tf_op jit(solution)/shard_map/while/body/eval_jaxpr/ppermute | solution.py:470
  222.5 3.1 %collective-permute-start.5 = (f32[64,128]{1,0:T(8,128)S(1)}, f32[64,128]{1,0:T(8,128)S(1)}, u32[]{:S(2)}, u32[]{:S(2)}) collective-permute-start(f32[64,128]{1,0:T(8,128)S(1)} %get-tuple-element.394.zh), channel_id=1, source_target_pairs={{0,7},{1,0},{2,1},{3,2},{4,3},{5,4},{6,5},{7,6},{8,15},{9,8},{10,9... | collective-permute-start | bytes 98312 | tf_op jit(solution)/shard_map/while/body/eval_jaxpr/ppermute | solution.py:470

commit v3 on v2

--- a/solution.py
+++ b/solution.py
@@ -244,39 +244,6 @@
         stack_ref[384:448, cols] = jnp.where(lane == 127, high, pltpu.roll(here, 127, 1))
 
 
-def maps_kernel(
-    count, cells, sums_ref, base_ref, cons_ref, fa, fb, xh, yl, yh, zl, zh,
-    kb_ref, map_ref, sel_ref, seln_ref, gw_ref, mode_ref, mom_ref, civ_ref, ginv_ref, gain_ref,
-    stack_ref,
-):
-    sums, base, cons = sums_ref[...], base_ref[...], cons_ref[...]
-    gain = (TIME_STEP / cells) * mmt(base, sums[136:152, 64:128])
-    gain_ref[...] = gain
-    grams, mode_rows, moments = symmetric(sums, gain, cons)
-    shifted_stack(1, stack_ref, fb, fa, xh, yl, yh, zl, zh)
-    sides = mm(jnp.concatenate(grams, axis=0), base)
-    sides = [sides[64 * w : 64 * w + 64] for w in range(7)]
-    stay = (1.0 - TIME_STEP) * sides[0]
-    for d in range(3):
-        stay = stay + TIME_STEP * (sides[2 * d + 2] - sides[2 * d + 1])
-    row = [stay] + [TIME_STEP * sides[2 * d + 1] for d in range(3)]
-    row += [-TIME_STEP * sides[2 * d + 2] for d in range(3)] + [TIME_STEP * mode_rows.T]
-    row = jnp.concatenate(row, axis=1) * (1.0 / count)
-    sel = mm(cons[120:152, 0:8], mm(moments, base) * (1.0 / count))
-    sel_ref[...] = sel
-    stack_ref[448:464, :] = features(sel, fb[...])
-    gw_ref[...] = jnp.concatenate(grams[1:], axis=1)
-    mode_ref[...] = mode_rows
-    mom_ref[...] = moments
-    _, civ = chol_inverse(grams[0] * (1.0 / count))
-    maps = mm(civ, row)
-    kb_ref[...] = mm(maps, stack_ref[...])
-    map_ref[...] = maps
-    civ_ref[...] = civ
-    ginv_ref[...] = mm(civ.T, civ) * (1.0 / count)
-    seln_ref[...] = mm(cons[120:152, 0:8], mmt(moments, civ) * (1.0 / count))
-
-
 def columns(fields, lane_at):
     lane = iota((RANK, 128), 1)
     out = jnp.zeros((RANK, 128), F32)
@@ -289,20 +256,45 @@
     return out
 
 
-def plane_kernel(
-    map_ref, sel_ref, fa, fb, xl, yl, yh, zl, zh, kb,
-    ka_ref, ylo_ref, yho_ref, zlo_ref, zho_ref, stack_ref,
+def maps_kernel(
+    count, cells, sums_ref, base_ref, cons_ref, fa, fb, xl, xh, yl, yh, zl, zh,
+    kb_ref, ka_ref, ylo_ref, yho_ref, zlo_ref, zho_ref,
+    seln_ref, gw_ref, mode_ref, mom_ref, civ_ref, ginv_ref, gain_ref, stack_ref, other_ref,
 ):
-    shifted_stack(0, stack_ref, fa, xl, fb, yl, yh, zl, zh)
-    stack_ref[448:464, :] = features(sel_ref[...], fa[...])
-    ka = mm(map_ref[...], stack_ref[...])
+    sums, base, cons = sums_ref[...], base_ref[...], cons_ref[...]
+    gain = (TIME_STEP / cells) * mmt(base, sums[136:152, 64:128])
+    gain_ref[...] = gain
+    grams, mode_rows, moments = symmetric(sums, gain, cons)
+    shifted_stack(1, stack_ref, fb, fa, xh, yl, yh, zl, zh)
+    shifted_stack(0, other_ref, fa, xl, fb, yl, yh, zl, zh)
+    sides = mm(jnp.concatenate(grams, axis=0), base)
+    sides = [sides[64 * w : 64 * w + 64] for w in range(7)]
+    stay = (1.0 - TIME_STEP) * sides[0]
+    for d in range(3):
+        stay = stay + TIME_STEP * (sides[2 * d + 2] - sides[2 * d + 1])
+    row = [stay] + [TIME_STEP * sides[2 * d + 1] for d in range(3)]
+    row += [-TIME_STEP * sides[2 * d + 2] for d in range(3)] + [TIME_STEP * mode_rows.T]
+    row = jnp.concatenate(row, axis=1) * (1.0 / count)
+    sel = mm(cons[120:152, 0:8], mm(moments, base) * (1.0 / count))
+    stack_ref[448:464, :] = features(sel, fb[...])
+    other_ref[448:464, :] = features(sel, fa[...])
+    gw_ref[...] = jnp.concatenate(grams[1:], axis=1)
+    mode_ref[...] = mode_rows
+    mom_ref[...] = moments
+    _, civ = chol_inverse(grams[0] * (1.0 / count))
+    maps = mm(civ, row)
+    kb = mm(maps, stack_ref[...])
+    ka = mm(maps, other_ref[...])
+    kb_ref[...] = kb
     ka_ref[...] = ka
-    kb = kb[...]
     n = ka.shape[1]
     ylo_ref[...] = jnp.concatenate([ka[:, n - 128 :], kb[:, n - 128 :]], axis=1)
     yho_ref[...] = jnp.concatenate([ka[:, :128], kb[:, :128]], axis=1)
     zlo_ref[...] = columns((ka, kb), 127)
     zho_ref[...] = columns((ka, kb), 0)
+    civ_ref[...] = civ
+    ginv_ref[...] = mm(civ.T, civ) * (1.0 / count)
+    seln_ref[...] = mm(cons[120:152, 0:8], mmt(moments, civ) * (1.0 / count))
 
 
 def inner_kernel(seln_ref, ka, kb, out_ref, stack_ref):
@@ -483,18 +475,12 @@
 
     def step(turn, carry):
         fa, fb, low, high, sums, rows, base, _ = carry
-        kb, maps, sel, seln, gw, mode_rows, moments, civ, ginv, gain = call(
+        kb, ka, yl, yh, zl, zh, seln, gw, mode_rows, moments, civ, ginv, gain = call(
             functools.partial(maps_kernel, count, cells),
-            [(RANK, half), (RANK, 464), (32, RANK), (32, RANK), (RANK, 384), (16, RANK), (8, RANK),
-             (RANK, RANK), (RANK, RANK), (RANK, 16)],
-            [(464, half)],
-            sums, base, cons, fa, fb, high[0], low[1], high[1], low[2], high[2],
-        )
-        ka, yl, yh, zl, zh = call(
-            plane_kernel,
-            [(RANK, half), (RANK, 256), (RANK, 256), (RANK, 128), (RANK, 128)],
-            [(464, half)],
-            maps, sel, fa, fb, low[0], low[1], high[1], low[2], high[2], kb,
+            [(RANK, half), (RANK, half), (RANK, 256), (RANK, 256), (RANK, 128), (RANK, 128),
+             (32, RANK), (RANK, 384), (16, RANK), (8, RANK), (RANK, RANK), (RANK, RANK), (RANK, 16)],
+            [(464, half), (464, half)],
+            sums, base, cons, fa, fb, low[0], high[0], low[1], high[1], low[2], high[2],
         )
         low = low_halo(kb, yl, zl)
         (part,) = call(inner_kernel, [(272, RANK)], [(272, 2 * half)], seln, ka, kb)

time: 232 us -> 233 us (level)
    pallas_call x14 -> x12, Pallas kernels: 45.5 us -> 45.2 us  [call(): pl.pallas_call(kernel, out_shape=shapes, in_specs=specs, out_specs=[pl.Bl...]
  transfers between devices with their start and end apart: 24 -> 24, of which waited for: 12 -> 12; matrix products, arithmetic and copies ran while one was open for 1% -> 1% of each run, Pallas kernels for 5% -> 4%
where the time goes in v3:
time: 233 us; the launch traced here: 232 us
  blocking collectives  87.3 us (37%)
  starting transfers between devices  60.5 us (26%)
  Pallas kernels  45.2 us (19%)
  waiting for transfers between devices  32.7 us (14%)
  local copies, waits for them, and re-layouts  5.37 us (2%)
    all_to_all x8, blocking collectives, swap(): return lax.all_to_all(chunks, axis, 0, 0, tiled=True)  87.3 us
    pallas_call x12, Pallas kernels, call(): pl.pallas_call(kernel, out_shape=shapes, in_specs=specs, out_specs=[pl.Bl...  45.2 us
    ppermute x18, starting transfers between devices, halo(): out.append(lax.ppermute(field, axis, route(axis, step)))  30.5 us
    all_to_all x6, starting transfers between devices, swap(): return lax.all_to_all(chunks, axis, 0, 0, tiled=True)  29.9 us
    all_to_all x6, waiting for transfers between devices, swap(): return lax.all_to_all(chunks, axis, 0, 0, tiled=True)  20.5 us
    ppermute x18, waiting for transfers between devices, halo(): out.append(lax.ppermute(field, axis, route(axis, step)))  12.2 us
  transfers between devices with their start and end apart: 24, of which 12 were waited for; matrix products, arithmetic and copies ran while one was open for 1% of the time, Pallas kernels for 4%

profile of v3, /device:TPU:1, one launch (start us, length us, event | category | flops | bytes accessed | tf_op | source)
XLA Modules:
  0.0 232.3 jit_solution(8883657564889906537)
XLA Ops:
  0.6 1.0 copy.82.rows_ref
  2.1 2.1 collective-permute-start.7
  4.3 2.3 %shard_map.67 = (f32[256,128]{1,0:T(8,128)}, f32[24,1024]{1,0:T(8,128)S(1)}) custom-call(f32[1,1]{1,0:T(1,128)} %bitcast.2.v1_ref, f32[64,1024]{1,0:T(8,128)S(1)} %copy.82.rows_ref), custom_call_target="tpu_custom_call" | custom-call | tf_op jit(solution)/shard_map/pallas_call | solution.py:398
  6.6 7.8 %all-to-all-start.6 = ((f32[32,8,128]{2,1,0:T(8,128)}), f32[32,8,128]{2,1,0:T(8,128)S(1)}, u32[]{:S(2)}, u32[]{:S(2)}) async-start(f32[32,8,128]{2,1,0:T(8,128)} %bitcast.3), calls=%async_computation.6 | async-start | bytes 262144 | tf_op jit(solution)/shard_map/all_to_all | solution.py:415
  14.8 3.1 %collective-permute-start.6 = (f32[64,1024]{1,0:T(8,128)S(1)}, f32[64,1024]{1,0:T(8,128)S(1)}, u32[]{:S(2)}, u32[]{:S(2)}) collective-permute-start(f32[64,1024]{1,0:T(8,128)S(1)} %bitcast.40), channel_id=1, source_target_pairs={{0,64},{64,128},{128,192},{192,0},{1,65},{65,129},{129,193},{193,1... | collective-permute-start | bytes 786440 | tf_op jit(solution)/shard_map/ppermute | solution.py:462
  17.9 4.0 %all-to-all-done.6 = f32[32,8,128]{2,1,0:T(8,128)S(1)} async-done(((f32[32,8,128]{2,1,0:T(8,128)}), f32[32,8,128]{2,1,0:T(8,128)S(1)}, u32[]{:S(2)}, u32[]{:S(2)}) %all-to-all-start.6) | async-done | bytes 131104 | tf_op jit(solution)/shard_map/all_to_all | solution.py:415
  21.9 0.7 broadcast_in_dim.12
  22.6 4.0 %all-to-all-start.7 = ((f32[32,8,128]{2,1,0:T(8,128)}), f32[32,8,128]{2,1,0:T(8,128)S(1)}, u32[]{:S(2)}, u32[]{:S(2)}) async-start(f32[32,8,128]{2,1,0:T(8,128)} %broadcast_in_dim.12), calls=%async_computation.7 | async-start | bytes 262144 | tf_op jit(solution)/shard_map/all_to_all | solution.py:415
  27.1 5.6 %collective-permute-start.11 = (f32[64,128]{0,1:T(8,128)S(1)}, f32[64,128]{0,1:T(8,128)S(1)}, u32[]{:S(2)}, u32[]{:S(2)}) collective-permute-start(f32[64,128]{0,1:T(8,128)S(1)} %concatenate.7), channel_id=1, source_target_pairs={{0,7},{1,0},{2,1},{3,2},{4,3},{5,4},{6,5},{7,6},{8,15},{9,8},{10,9... | collective-permute-start | bytes 98312 | tf_op jit(solution)/shard_map/ppermute | solution.py:462
  32.8 3.5 %collective-permute-start.10 = (f32[64,256]{1,0:T(8,128)S(1)}, f32[64,256]{1,0:T(8,128)S(1)}, u32[]{:S(2)}, u32[]{:S(2)}) collective-permute-start(f32[64,256]{1,0:T(8,128)S(1)} %bitcast.50), channel_id=1, source_target_pairs={{0,56},{8,0},{16,8},{24,16},{32,24},{40,32},{48,40},{56,48},{1,57}... | collective-permute-start | bytes 196616 | tf_op jit(solution)/shard_map/ppermute | solution.py:462
  37.4 3.5 %collective-permute-done.8 = f32[64,128]{0,1:T(8,128)S(1)} collective-permute-done((f32[64,128]{0,1:T(8,128)S(1)}, f32[64,128]{0,1:T(8,128)S(1)}, u32[]{:S(2)}, u32[]{:S(2)}) %collective-permute-start.8) | collective-permute-done | bytes 32800 | tf_op jit(solution)/shard_map/ppermute | solution.py:462
  41.1 186.6 %while.33 = (s32[]{:T(128)}, f32[64,1024]{1,0:T(8,128)S(1)}, f32[64,1024]{1,0:T(8,128)S(1)}, f32[64,1024]{1,0:T(8,128)S(1)}, f32[64,256]{1,0:T(8,128)S(1)}, /*in...) while((s32[]{:T(128)}, f32[64,1024]{1,0:T(8,128)S(1)}, ...), condition=%wide.region_6.7_spmd.clone, body=%wide.region_1.6_spmd.sunk.clone.sunk | while | flops 58370 | bytes 5595621 | solution.py:504
  41.3 6.6 %eval_jaxpr.5 = (f32[64,1024]{1,0:T(8,128)S(1)}, f32[64,1024]{1,0:T(8,128)S(1)}, f32[64,256]{1,0:T(8,128)S(1)}, f32[64,256]{1,0:T(8,128)S(1)}, f32[64,128]{1,0:T...) custom-call(f32[256,128]{1,0:T(8,128)S(1)} %get-tuple-element.422.su, ...), custom_call_target="tpu_custom_call" | custom-call | tf_op jit(solution)/shard_map/while/body/eval_jaxpr/pallas_call | solution.py:398
  47.9 4.4 %collective-permute-start = (f32[64,1024]{1,0:T(8,128)S(1)}, f32[64,1024]{1,0:T(8,128)S(1)}, u32[]{:S(2)}, u32[]{:S(2)}) collective-permute-start(f32[64,1024]{1,0:T(8,128)S(1)} %get-tuple-element.433.kb), channel_id=1, source_target_pairs={{0,64},{64,128},{128,192},{192,0},{1,65},{65,129},{129,193},{193,1... | collective-permute-start | bytes 786440 | tf_op jit(solution)/shard_map/while/body/eval_jaxpr/ppermute | solution.py:462
  52.3 2.2 eval_jaxpr.6.part_ref
  54.5 2.1 collective-permute-done.2.zl
  56.6 1.0 collective-permute-done.1.yl
  58.1 12.4 %all_to_all.58 = f32[32,4,128]{2,1,0:T(4,128)S(1)} all-to-all(f32[32,4,128]{2,1,0:T(4,128)S(1)} %bitcast.36), channel_id=1, replica_groups=mesh['bx'=4,'by'=8,'bz'=8] {'bx','by'}, dimensions={0} | all-to-all | bytes 131072 | tf_op jit(solution)/shard_map/while/body/eval_jaxpr/all_to_all | solution.py:415
  70.5 10.3 %all_to_all.59 = f32[8,4,128]{2,1,0:T(4,128)S(1)} all-to-all(f32[8,4,128]{2,1,0:T(4,128)S(1)} %broadcast_in_dim.48), channel_id=1, replica_groups=mesh['bx'=4,'by'=8,'bz'=8] {'bz'}, dimensions={0} | all-to-all | bytes 32768 | tf_op jit(solution)/shard_map/while/body/eval_jaxpr/all_to_all | solution.py:415
  80.8 12.3 %all_to_all.60 = f32[32,4,128]{2,1,0:T(4,128)S(1)} all-to-all(f32[32,4,128]{2,1,0:T(4,128)S(1)} %broadcast_in_dim.49), channel_id=1, replica_groups=mesh['bx'=4,'by'=8,'bz'=8] {'bx','by'}, dimensions={0} | all-to-all | bytes 131072 | tf_op jit(solution)/shard_map/while/body/eval_jaxpr/all_to_all | solution.py:415
  93.1 8.4 %eval_jaxpr.8 = (f32[256,128]{1,0:T(8,128)}, f32[64,1024]{1,0:T(8,128)S(1)}, f32[64,64]{1,0:T(8,128)S(1)}) custom-call(f32[1,1]{1,0:T(1,128)} %get-tuple-element.444.v1_ref, f32[128,128]{1,0:T(8,128)S(1)} %bitcast.37, f32[64,1024]{1,0:T(8,128)S(1)} %get-tuple-element.432.ka, f32[64,1024]{1,0:T(8,128)S(1)} %get-tuple-element.433.kb, ...), custom_call_target="tpu_custom_call", output_to_operand_aliasing={{1}: (4, {})} | custom-call | tf_op jit(solution)/shard_map/while/body/eval_jaxpr/pallas_call | solution.py:398
  101.5 3.9 %all-to-all-start.3 = ((f32[32,8,128]{2,1,0:T(8,128)}), f32[32,8,128]{2,1,0:T(8,128)S(1)}, u32[]{:S(2)}, u32[]{:S(2)}) async-start(f32[32,8,128]{2,1,0:T(8,128)} %bitcast.34), calls=%async_computation.3 | async-start | bytes 262144 | tf_op jit(solution)/shard_map/while/body/eval_jaxpr/all_to_all | solution.py:415
  105.8 7.3 %all-to-all-done.3 = f32[32,8,128]{2,1,0:T(8,128)S(1)} async-done(((f32[32,8,128]{2,1,0:T(8,128)}), f32[32,8,128]{2,1,0:T(8,128)S(1)}, u32[]{:S(2)}, u32[]{:S(2)}) %all-to-all-start.3) | async-done | bytes 131104 | tf_op jit(solution)/shard_map/while/body/eval_jaxpr/all_to_all | solution.py:415
  113.1 9.2 %all_to_all.61 = f32[8,8,128]{2,1,0:T(8,128)S(1)} all-to-all(f32[8,8,128]{2,1,0:T(8,128)S(1)} %broadcast_in_dim.50), channel_id=1, replica_groups=mesh['bx'=4,'by'=8,'bz'=8] {'bz'}, dimensions={0} | all-to-all | bytes 65536 | tf_op jit(solution)/shard_map/while/body/eval_jaxpr/all_to_all | solution.py:415
  123.1 5.1 %all-to-all-start.5 = ((f32[32,8,128]{2,1,0:T(8,128)}), f32[32,8,128]{2,1,0:T(8,128)S(1)}, u32[]{:S(2)}, u32[]{:S(2)}) async-start(f32[32,8,128]{2,1,0:T(8,128)} %broadcast_in_dim.51), calls=%async_computation.5 | async-start | bytes 262144 | tf_op jit(solution)/shard_map/while/body/eval_jaxpr/all_to_all | solution.py:415
  128.2 3.6 %collective-permute-start.4 = (f32[64,256]{1,0:T(8,128)S(1)}, f32[64,256]{1,0:T(8,128)S(1)}, u32[]{:S(2)}, u32[]{:S(2)}) collective-permute-start(f32[64,256]{1,0:T(8,128)S(1)} %get-tuple-element.383.yh), channel_id=1, source_target_pairs={{0,56},{8,0},{16,8},{24,16},{32,24},{40,32},{48,40},{56,48},{1,57}... | collective-permute-start | bytes 196616 | tf_op jit(solution)/shard_map/while/body/eval_jaxpr/ppermute | solution.py:462
  132.0 1.5 eval_jaxpr.9
  133.5 1.4 collective-permute-done.5
  134.9 1.0 all-to-all-done.5
  135.9 6.6 %eval_jaxpr.5 = (f32[64,1024]{1,0:T(8,128)S(1)}, f32[64,1024]{1,0:T(8,128)S(1)}, f32[64,256]{1,0:T(8,128)S(1)}, f32[64,256]{1,0:T(8,128)S(1)}, f32[64,128]{1,0:T...) custom-call(f32[256,128]{1,0:T(8,128)S(1)} %get-tuple-element.422.su, ...), custom_call_target="tpu_custom_call" | custom-call | tf_op jit(solution)/shard_map/while/body/eval_jaxpr/pallas_call | solution.py:398
  142.4 2.9 %collective-permute-start = (f32[64,1024]{1,0:T(8,128)S(1)}, f32[64,1024]{1,0:T(8,128)S(1)}, u32[]{:S(2)}, u32[]{:S(2)}) collective-permute-start(f32[64,1024]{1,0:T(8,128)S(1)} %get-tuple-element.433.kb), channel_id=1, source_target_pairs={{0,64},{64,128},{128,192},{192,0},{1,65},{65,129},{129,193},{193,1... | collective-permute-start | bytes 786440 | tf_op jit(solution)/shard_map/while/body/eval_jaxpr/ppermute | solution.py:462
  145.6 2.1 eval_jaxpr.6.part_ref
  147.8 1.8 collective-permute-done.2.zl
  149.6 1.0 collective-permute-done.1.yl
  151.1 12.4 %all_to_all.58 = f32[32,4,128]{2,1,0:T(4,128)S(1)} all-to-all(f32[32,4,128]{2,1,0:T(4,128)S(1)} %bitcast.36), channel_id=1, replica_groups=mesh['bx'=4,'by'=8,'bz'=8] {'bx','by'}, dimensions={0} | all-to-all | bytes 131072 | tf_op jit(solution)/shard_map/while/body/eval_jaxpr/all_to_all | solution.py:415
  163.5 9.2 %all_to_all.59 = f32[8,4,128]{2,1,0:T(4,128)S(1)} all-to-all(f32[8,4,128]{2,1,0:T(4,128)S(1)} %broadcast_in_dim.48), channel_id=1, replica_groups=mesh['bx'=4,'by'=8,'bz'=8] {'bz'}, dimensions={0} | all-to-all | bytes 32768 | tf_op jit(solution)/shard_map/while/body/eval_jaxpr/all_to_all | solution.py:415
  172.7 12.3 %all_to_all.60 = f32[32,4,128]{2,1,0:T(4,128)S(1)} all-to-all(f32[32,4,128]{2,1,0:T(4,128)S(1)} %broadcast_in_dim.49), channel_id=1, replica_groups=mesh['bx'=4,'by'=8,'bz'=8] {'bx','by'}, dimensions={0} | all-to-all | bytes 131072 | tf_op jit(solution)/shard_map/while/body/eval_jaxpr/all_to_all | solution.py:415
  185.0 8.4 %eval_jaxpr.8 = (f32[256,128]{1,0:T(8,128)}, f32[64,1024]{1,0:T(8,128)S(1)}, f32[64,64]{1,0:T(8,128)S(1)}) custom-call(f32[1,1]{1,0:T(1,128)} %get-tuple-element.444.v1_ref, f32[128,128]{1,0:T(8,128)S(1)} %bitcast.37, f32[64,1024]{1,0:T(8,128)S(1)} %get-tuple-element.432.ka, f32[64,1024]{1,0:T(8,128)S(1)} %get-tuple-element.433.kb, ...), custom_call_target="tpu_custom_call", output_to_operand_aliasing={{1}: (4, {})} | custom-call | tf_op jit(solution)/shard_map/while/body/eval_jaxpr/pallas_call | solution.py:398
  193.4 4.0 %all-to-all-start.3 = ((f32[32,8,128]{2,1,0:T(8,128)}), f32[32,8,128]{2,1,0:T(8,128)S(1)}, u32[]{:S(2)}, u32[]{:S(2)}) async-start(f32[32,8,128]{2,1,0:T(8,128)} %bitcast.34), calls=%async_computation.3 | async-start | bytes 262144 | tf_op jit(solution)/shard_map/while/body/eval_jaxpr/all_to_all | solution.py:415
  197.7 7.3 %all-to-all-done.3 = f32[32,8,128]{2,1,0:T(8,128)S(1)} async-done(((f32[32,8,128]{2,1,0:T(8,128)}), f32[32,8,128]{2,1,0:T(8,128)S(1)}, u32[]{:S(2)}, u32[]{:S(2)}) %all-to-all-start.3) | async-done | bytes 131104 | tf_op jit(solution)/shard_map/while/body/eval_jaxpr/all_to_all | solution.py:415
  205.0 9.2 %all_to_all.61 = f32[8,8,128]{2,1,0:T(8,128)S(1)} all-to-all(f32[8,8,128]{2,1,0:T(8,128)S(1)} %broadcast_in_dim.50), channel_id=1, replica_groups=mesh['bx'=4,'by'=8,'bz'=8] {'bz'}, dimensions={0} | all-to-all | bytes 65536 | tf_op jit(solution)/shard_map/while/body/eval_jaxpr/all_to_all | solution.py:415
  214.3 0.7 broadcast_in_dim.51
  214.9 5.1 %all-to-all-start.5 = ((f32[32,8,128]{2,1,0:T(8,128)}), f32[32,8,128]{2,1,0:T(8,128)S(1)}, u32[]{:S(2)}, u32[]{:S(2)}) async-start(f32[32,8,128]{2,1,0:T(8,128)} %broadcast_in_dim.51), calls=%async_computation.5 | async-start | bytes 262144 | tf_op jit(solution)/shard_map/while/body/eval_jaxpr/all_to_all | solution.py:415
  220.1 3.6 %collective-permute-start.4 = (f32[64,256]{1,0:T(8,128)S(1)}, f32[64,256]{1,0:T(8,128)S(1)}, u32[]{:S(2)}, u32[]{:S(2)}) collective-permute-start(f32[64,256]{1,0:T(8,128)S(1)} %get-tuple-element.383.yh), channel_id=1, source_target_pairs={{0,56},{8,0},{16,8},{24,16},{32,24},{40,32},{48,40},{56,48},{1,57}... | collective-permute-start | bytes 196616 | tf_op jit(solution)/shard_map/while/body/eval_jaxpr/ppermute | solution.py:462
  223.8 1.5 eval_jaxpr.9
  225.3 1.4 collective-permute-done.5
  226.8 1.0 all-to-all-done.5
  227.7 4.6 %shard_map.68 = (f32[64,64]{1,0:T(8,128)}, f32[64,1024]{1,0:T(8,128)}) custom-call(f32[256,128]{1,0:T(8,128)S(1)} %get-tuple-element.110.sums_ref, f32[64,64]{1,0:T(8,128)S(1)} %get-tuple-element.111.cxi_ref, f32[64,1024]{1,0:T(8,128)S(1)} %get-tuple-element.112.rows_ref, f32[24,1024]{1,0:T(8,128)S(1)} %get-tuple-element.468, f32[160,16]{1,0:T(8,128)S(1)} %get-tuple-element.458), custom_call_target="tpu_custom_call" | custom-call | tf_op jit(solution)/shard_map/pallas_call | solution.py:398
  (65 shorter events, 6.0 us)
Async XLA Ops:
  0.6 1.1 copy-start.1
  2.1 38.9 %collective-permute-start.7 = (f32[64,256]{1,0:T(8,128)S(1)}, f32[64,256]{1,0:T(8,128)S(1)}, u32[]{:S(2)}, u32[]{:S(2)}) collective-permute-start(f32[64,256]{1,0:T(8,128)S(1)} %bitcast.49), channel_id=1, source_target_pairs={{0,8},{8,16},{16,24},{24,32},{32,40},{40,48},{48,56},{56,0},{1,9},... | collective-permute-start | bytes 196616 | tf_op jit(solution)/shard_map/ppermute | solution.py:462
  6.6 15.3 %all-to-all-start.6 = ((f32[32,8,128]{2,1,0:T(8,128)}), f32[32,8,128]{2,1,0:T(8,128)S(1)}, u32[]{:S(2)}, u32[]{:S(2)}) async-start(f32[32,8,128]{2,1,0:T(8,128)} %bitcast.3), calls=%async_computation.6 | async-start | bytes 262144 | tf_op jit(solution)/shard_map/all_to_all | solution.py:415
  14.4 26.6 %collective-permute-start.9 = (f32[64,1024]{1,0:T(8,128)S(1)}, f32[64,1024]{1,0:T(8,128)S(1)}, u32[]{:S(2)}, u32[]{:S(2)}) collective-permute-start(f32[64,1024]{1,0:T(8,128)S(1)} %bitcast.38), channel_id=1, source_target_pairs={{0,192},{64,0},{128,64},{192,128},{1,193},{65,1},{129,65},{193,129... | collective-permute-start | bytes 786440 | tf_op jit(solution)/shard_map/ppermute | solution.py:462
  14.8 26.3 %collective-permute-start.6 = (f32[64,1024]{1,0:T(8,128)S(1)}, f32[64,1024]{1,0:T(8,128)S(1)}, u32[]{:S(2)}, u32[]{:S(2)}) collective-permute-start(f32[64,1024]{1,0:T(8,128)S(1)} %bitcast.40), channel_id=1, source_target_pairs={{0,64},{64,128},{128,192},{192,0},{1,65},{65,129},{129,193},{193,1... | collective-permute-start | bytes 786440 | tf_op jit(solution)/shard_map/ppermute | solution.py:462
  22.6 18.4 %all-to-all-start.7 = ((f32[32,8,128]{2,1,0:T(8,128)}), f32[32,8,128]{2,1,0:T(8,128)S(1)}, u32[]{:S(2)}, u32[]{:S(2)}) async-start(f32[32,8,128]{2,1,0:T(8,128)} %broadcast_in_dim.12), calls=%async_computation.7 | async-start | bytes 262144 | tf_op jit(solution)/shard_map/all_to_all | solution.py:415
  27.1 9.4 %collective-permute-start.11 = (f32[64,128]{0,1:T(8,128)S(1)}, f32[64,128]{0,1:T(8,128)S(1)}, u32[]{:S(2)}, u32[]{:S(2)}) collective-permute-start(f32[64,128]{0,1:T(8,128)S(1)} %concatenate.7), channel_id=1, source_target_pairs={{0,7},{1,0},{2,1},{3,2},{4,3},{5,4},{6,5},{7,6},{8,15},{9,8},{10,9... | collective-permute-start | bytes 98312 | tf_op jit(solution)/shard_map/ppermute | solution.py:462
  32.8 8.3 %collective-permute-start.10 = (f32[64,256]{1,0:T(8,128)S(1)}, f32[64,256]{1,0:T(8,128)S(1)}, u32[]{:S(2)}, u32[]{:S(2)}) collective-permute-start(f32[64,256]{1,0:T(8,128)S(1)} %bitcast.50), channel_id=1, source_target_pairs={{0,56},{8,0},{16,8},{24,16},{32,24},{40,32},{48,40},{56,48},{1,57}... | collective-permute-start | bytes 196616 | tf_op jit(solution)/shard_map/ppermute | solution.py:462
  36.5 0.8 copy-start.2
  36.6 4.4 %collective-permute-start.8 = (f32[64,128]{0,1:T(8,128)S(1)}, f32[64,128]{0,1:T(8,128)S(1)}, u32[]{:S(2)}, u32[]{:S(2)}) collective-permute-start(f32[64,128]{0,1:T(8,128)S(1)} %concatenate.6), channel_id=1, source_target_pairs={{0,1},{1,2},{2,3},{3,4},{4,5},{5,6},{6,7},{7,0},{8,9},{9,10},{10,1... | collective-permute-start | bytes 98312 | tf_op jit(solution)/shard_map/ppermute | solution.py:462
  37.4 3.7 %copy-start = (f32[160,16]{1,0:T(8,128)S(1)}, f32[160,16]{1,0:T(8,128)}, u32[]{:S(2)}) copy-start(f32[160,16]{1,0:T(8,128)} %constant.53.clone.cons_ref) | copy-start | bytes 30724
  47.9 9.7 %collective-permute-start = (f32[64,1024]{1,0:T(8,128)S(1)}, f32[64,1024]{1,0:T(8,128)S(1)}, u32[]{:S(2)}, u32[]{:S(2)}) collective-permute-start(f32[64,1024]{1,0:T(8,128)S(1)} %get-tuple-element.433.kb), channel_id=1, source_target_pairs={{0,64},{64,128},{128,192},{192,0},{1,65},{65,129},{129,193},{193,1... | collective-permute-start | bytes 786440 | tf_op jit(solution)/shard_map/while/body/eval_jaxpr/ppermute | solution.py:462
  52.3 5.2 %collective-permute-start.1 = (f32[64,256]{1,0:T(8,128)S(1)}, f32[64,256]{1,0:T(8,128)S(1)}, u32[]{:S(2)}, u32[]{:S(2)}) collective-permute-start(f32[64,256]{1,0:T(8,128)S(1)} %get-tuple-element.381), channel_id=1, source_target_pairs={{0,8},{8,16},{16,24},{24,32},{32,40},{40,48},{48,56},{56,0},{1,9},... | collective-permute-start | bytes 196616 | tf_op jit(solution)/shard_map/while/body/eval_jaxpr/ppermute | solution.py:462
  52.3 4.3 %collective-permute-start.2 = (f32[64,128]{1,0:T(8,128)S(1)}, f32[64,128]{1,0:T(8,128)S(1)}, u32[]{:S(2)}, u32[]{:S(2)}) collective-permute-start(f32[64,128]{1,0:T(8,128)S(1)} %get-tuple-element.382), channel_id=1, source_target_pairs={{0,1},{1,2},{2,3},{3,4},{4,5},{5,6},{6,7},{7,0},{8,9},{9,10},{10,1... | collective-permute-start | bytes 98312 | tf_op jit(solution)/shard_map/while/body/eval_jaxpr/ppermute | solution.py:462
  101.5 11.6 %all-to-all-start.3 = ((f32[32,8,128]{2,1,0:T(8,128)}), f32[32,8,128]{2,1,0:T(8,128)S(1)}, u32[]{:S(2)}, u32[]{:S(2)}) async-start(f32[32,8,128]{2,1,0:T(8,128)} %bitcast.34), calls=%async_computation.3 | async-start | bytes 262144 | tf_op jit(solution)/shard_map/while/body/eval_jaxpr/all_to_all | solution.py:415
  105.5 29.4 %collective-permute-start.3 = (f32[64,1024]{1,0:T(8,128)S(1)}, f32[64,1024]{1,0:T(8,128)S(1)}, u32[]{:S(2)}, u32[]{:S(2)}) collective-permute-start(f32[64,1024]{1,0:T(8,128)S(1)} %get-tuple-element.432.ka), channel_id=1, source_target_pairs={{0,192},{64,0},{128,64},{192,128},{1,193},{65,1},{129,65},{193,129... | collective-permute-start | bytes 786440 | tf_op jit(solution)/shard_map/while/body/eval_jaxpr/ppermute | solution.py:462
  123.1 12.8 %all-to-all-start.5 = ((f32[32,8,128]{2,1,0:T(8,128)}), f32[32,8,128]{2,1,0:T(8,128)S(1)}, u32[]{:S(2)}, u32[]{:S(2)}) async-start(f32[32,8,128]{2,1,0:T(8,128)} %broadcast_in_dim.51), calls=%async_computation.5 | async-start | bytes 262144 | tf_op jit(solution)/shard_map/while/body/eval_jaxpr/all_to_all | solution.py:415
  128.2 6.6 %collective-permute-start.4 = (f32[64,256]{1,0:T(8,128)S(1)}, f32[64,256]{1,0:T(8,128)S(1)}, u32[]{:S(2)}, u32[]{:S(2)}) collective-permute-start(f32[64,256]{1,0:T(8,128)S(1)} %get-tuple-element.383.yh), channel_id=1, source_target_pairs={{0,56},{8,0},{16,8},{24,16},{32,24},{40,32},{48,40},{56,48},{1,57}... | collective-permute-start | bytes 196616 | tf_op jit(solution)/shard_map/while/body/eval_jaxpr/ppermute | solution.py:462
  131.8 3.1 %collective-permute-start.5 = (f32[64,128]{1,0:T(8,128)S(1)}, f32[64,128]{1,0:T(8,128)S(1)}, u32[]{:S(2)}, u32[]{:S(2)}) collective-permute-start(f32[64,128]{1,0:T(8,128)S(1)} %get-tuple-element.384.zh), channel_id=1, source_target_pairs={{0,7},{1,0},{2,1},{3,2},{4,3},{5,4},{6,5},{7,6},{8,15},{9,8},{10,9... | collective-permute-start | bytes 98312 | tf_op jit(solution)/shard_map/while/body/eval_jaxpr/ppermute | solution.py:462
  142.4 8.1 %collective-permute-start = (f32[64,1024]{1,0:T(8,128)S(1)}, f32[64,1024]{1,0:T(8,128)S(1)}, u32[]{:S(2)}, u32[]{:S(2)}) collective-permute-start(f32[64,1024]{1,0:T(8,128)S(1)} %get-tuple-element.433.kb), channel_id=1, source_target_pairs={{0,64},{64,128},{128,192},{192,0},{1,65},{65,129},{129,193},{193,1... | collective-permute-start | bytes 786440 | tf_op jit(solution)/shard_map/while/body/eval_jaxpr/ppermute | solution.py:462
  145.3 5.2 %collective-permute-start.1 = (f32[64,256]{1,0:T(8,128)S(1)}, f32[64,256]{1,0:T(8,128)S(1)}, u32[]{:S(2)}, u32[]{:S(2)}) collective-permute-start(f32[64,256]{1,0:T(8,128)S(1)} %get-tuple-element.381), channel_id=1, source_target_pairs={{0,8},{8,16},{16,24},{24,32},{32,40},{40,48},{48,56},{56,0},{1,9},... | collective-permute-start | bytes 196616 | tf_op jit(solution)/shard_map/while/body/eval_jaxpr/ppermute | solution.py:462
  145.3 4.3 %collective-permute-start.2 = (f32[64,128]{1,0:T(8,128)S(1)}, f32[64,128]{1,0:T(8,128)S(1)}, u32[]{:S(2)}, u32[]{:S(2)}) collective-permute-start(f32[64,128]{1,0:T(8,128)S(1)} %get-tuple-element.382), channel_id=1, source_target_pairs={{0,1},{1,2},{2,3},{3,4},{4,5},{5,6},{6,7},{7,0},{8,9},{9,10},{10,1... | collective-permute-start | bytes 98312 | tf_op jit(solution)/shard_map/while/body/eval_jaxpr/ppermute | solution.py:462
  193.4 11.6 %all-to-all-start.3 = ((f32[32,8,128]{2,1,0:T(8,128)}), f32[32,8,128]{2,1,0:T(8,128)S(1)}, u32[]{:S(2)}, u32[]{:S(2)}) async-start(f32[32,8,128]{2,1,0:T(8,128)} %bitcast.34), calls=%async_computation.3 | async-start | bytes 262144 | tf_op jit(solution)/shard_map/while/body/eval_jaxpr/all_to_all | solution.py:415
  197.3 29.4 %collective-permute-start.3 = (f32[64,1024]{1,0:T(8,128)S(1)}, f32[64,1024]{1,0:T(8,128)S(1)}, u32[]{:S(2)}, u32[]{:S(2)}) collective-permute-start(f32[64,1024]{1,0:T(8,128)S(1)} %get-tuple-element.432.ka), channel_id=1, source_target_pairs={{0,192},{64,0},{128,64},{192,128},{1,193},{65,1},{129,65},{193,129... | collective-permute-start | bytes 786440 | tf_op jit(solution)/shard_map/while/body/eval_jaxpr/ppermute | solution.py:462
  214.9 12.8 %all-to-all-start.5 = ((f32[32,8,128]{2,1,0:T(8,128)}), f32[32,8,128]{2,1,0:T(8,128)S(1)}, u32[]{:S(2)}, u32[]{:S(2)}) async-start(f32[32,8,128]{2,1,0:T(8,128)} %broadcast_in_dim.51), calls=%async_computation.5 | async-start | bytes 262144 | tf_op jit(solution)/shard_map/while/body/eval_jaxpr/all_to_all | solution.py:415
  220.1 6.6 %collective-permute-start.4 = (f32[64,256]{1,0:T(8,128)S(1)}, f32[64,256]{1,0:T(8,128)S(1)}, u32[]{:S(2)}, u32[]{:S(2)}) collective-permute-start(f32[64,256]{1,0:T(8,128)S(1)} %get-tuple-element.383.yh), channel_id=1, source_target_pairs={{0,56},{8,0},{16,8},{24,16},{32,24},{40,32},{48,40},{56,48},{1,57}... | collective-permute-start | bytes 196616 | tf_op jit(solution)/shard_map/while/body/eval_jaxpr/ppermute | solution.py:462
  223.7 3.1 %collective-permute-start.5 = (f32[64,128]{1,0:T(8,128)S(1)}, f32[64,128]{1,0:T(8,128)S(1)}, u32[]{:S(2)}, u32[]{:S(2)}) collective-permute-start(f32[64,128]{1,0:T(8,128)S(1)} %get-tuple-element.384.zh), channel_id=1, source_target_pairs={{0,7},{1,0},{2,1},{3,2},{4,3},{5,4},{6,5},{7,6},{8,15},{9,8},{10,9... | collective-permute-start | bytes 98312 | tf_op jit(solution)/shard_map/while/body/eval_jaxpr/ppermute | solution.py:462
